TPU v7x, 32 devices: a whole 2x2x4 slice. The times are simulated.
32 devices in a mesh: kv: 4 (over y, x), seq: 8 (over z, core).
Axes of the slice: x: 2, y: 2, z: 4, core: 2. Of those that a mesh axis runs over, the one named last changes fastest.
Arguments:
- queries: bfloat16 [1024, 12288], P('seq', 'kv'), may hold values from -400 to 400
- cache_keys: bfloat16 [8192, 768], P('seq', 'kv'), may hold values from -6 to 6
- cache_values: bfloat16 [8192, 512], P('seq', 'kv'), may hold values from -6 to 6
- incoming_keys: bfloat16 [1024, 768], P('seq', 'kv'), may hold values from -6 to 6
- new_values: bfloat16 [1024, 512], P('seq', 'kv'), may hold values from -6 to 6
- comp_key_weight: bfloat16 [6144, 192], P('kv'), may hold values from -0.078125 to 0.078125
- comp_value_weight: bfloat16 [4096, 128], P('kv'), may hold values from -0.09375 to 0.09375
- select_blocks: int32 [32, 4, 16], P('seq', 'kv'), may hold values from 0 to 127, as said below
- gate_weight: bfloat16 [64, 192, 3], P('kv'), may hold values from -0.4375 to 0.4375
Outputs:
- attended: bfloat16 [1024, 8192], P('seq', 'kv')
Inputs may be any that keep to these rules, and one draw needn't show every extreme that they name: `select_blocks`: each row names 16 different blocks. For each KV group, the rows of one device of seq (4 tiles) name blocks of any one cache shard (the 16 blocks of one index of seq) at most 16 times in all, and in every draw the rows of every device name one shard's blocks exactly 16 times.
All inputs are finite; a program needn't handle non-finite values.
Results may differ from a plain program's by a relative error of at most 0.012.
Values may be sent and summed in bfloat16 or wider, within the bound.
A program may use at most 128 MiB of HBM per device.

v0:
```python
import jax
import jax.numpy as jnp
from jax import lax
from jax.sharding import PartitionSpec as P

CMP_STRIDE = 16
SEL_BLOCK = 64
WINDOW = 512


MASKED = -1e30


def passed_along(block, axis, distance):
    devices = range(lax.axis_size(axis))
    route = [((i - distance) % len(devices), i) for i in devices]
    return lax.ppermute(block, axis, route)


def from_behind(x, axis, by):
    peers = lax.axis_size(axis)
    pairs = [(i, i + by) for i in range(peers) if 0 <= i + by < peers]
    return lax.ppermute(x, axis, pairs)


def pack_rows(keys, values):
    return jnp.concatenate([keys.reshape(-1), values.reshape(-1)])


def unpack_rows(flat, count, key_width, value_width):
    keys = flat[: count * key_width].reshape(count, key_width)
    values = flat[count * key_width : count * (key_width + value_width)].reshape(count, value_width)
    return (keys, values)


def finish_rows(scores, values):
    top = jnp.max(scores, axis=-1, keepdims=True)
    weights = jnp.exp(scores - top)
    total = jnp.sum(weights, axis=-1, keepdims=True)
    mixed = jnp.matmul(weights.astype(jnp.bfloat16), values, preferred_element_type=jnp.float32)
    return mixed / total


def shards(
    queries,
    cache_keys,
    cache_values,
    incoming_keys,
    new_values,
    comp_key_weight,
    comp_value_weight,
    select_blocks,
    gate_weight,
):
    heads, key_width, _ = gate_weight.shape
    value_width = cache_values.shape[1]
    query_count = queries.shape[0]
    cache_count = cache_keys.shape[0]
    ranks = lax.axis_size("seq")
    place = lax.axis_index("seq")
    scale = key_width ** (-0.5)
    rows = queries.reshape(query_count * heads, key_width)
    row_total = rows.shape[0]
    stretch_pos = place * query_count + jnp.arange(query_count, dtype=jnp.int32)
    lookback_length = -(-WINDOW // query_count)
    weight_keys, weight_values = (
        lax.all_gather(comp_key_weight, "kv", axis=0, tiled=True),
        lax.all_gather(comp_value_weight, "kv", axis=0, tiled=True),
    )
    tail_pack = pack_rows(cache_keys[cache_count - WINDOW :], cache_values[cache_count - WINDOW :])
    moved_tail = passed_along(tail_pack, "seq", 1)
    before_keys, before_values = unpack_rows(moved_tail, WINDOW, key_width, value_width)
    edge_keys = before_keys[WINDOW - CMP_STRIDE :]
    edge_values = before_values[WINDOW - CMP_STRIDE :]
    held_tail = jnp.where(place == 0, moved_tail, jnp.zeros_like(moved_tail))
    tail_size = held_tail.shape[0]
    tail_flat = held_tail
    near_keys = []
    near_values = []
    nearby_positions = []
    near_valid = []
    own = pack_rows(incoming_keys, new_values)
    own_size = own.shape[0]
    for back in range(lookback_length, 0, -1):
        moved = from_behind(jnp.concatenate([own, held_tail]), "seq", back)
        got_keys, got_values = unpack_rows(moved, query_count, key_width, value_width)
        tail_flat = jnp.where(place == back, moved[own_size : own_size + tail_size], tail_flat)
        near_keys.append(got_keys)
        near_values.append(got_values)
        nearby_positions.append(
            (place - back) * query_count + jnp.arange(query_count, dtype=jnp.int32)
        )
        near_valid.append(jnp.broadcast_to(place >= back, (query_count,)))
    tail_keys, tail_values = unpack_rows(tail_flat, WINDOW, key_width, value_width)
    near_keys.append(tail_keys)
    near_values.append(tail_values)
    nearby_positions.append(jnp.arange(WINDOW, dtype=jnp.int32) - WINDOW)
    near_valid.append(jnp.ones((WINDOW,), dtype=bool))
    near_keys.append(incoming_keys)
    near_values.append(new_values)
    nearby_positions.append(stretch_pos)
    near_valid.append(jnp.ones((query_count,), dtype=bool))
    half_keys = CMP_STRIDE * key_width
    half_values = CMP_STRIDE * value_width
    lead_keys = jnp.concatenate([edge_keys, cache_keys[: cache_count - CMP_STRIDE]]).reshape(
        -1, half_keys
    )
    lead_values = jnp.concatenate([edge_values, cache_values[: cache_count - CMP_STRIDE]]).reshape(
        -1, half_values
    )
    comp_keys = (
        jnp.dot(lead_keys, weight_keys[:half_keys], preferred_element_type=jnp.float32)
        + jnp.dot(
            cache_keys.reshape(-1, half_keys),
            weight_keys[half_keys:],
            preferred_element_type=jnp.float32,
        )
    ).astype(jnp.bfloat16)
    comp_values = (
        jnp.dot(lead_values, weight_values[:half_values], preferred_element_type=jnp.float32)
        + jnp.dot(
            cache_values.reshape(-1, half_values),
            weight_values[half_values:],
            preferred_element_type=jnp.float32,
        )
    ).astype(jnp.bfloat16)
    start = jnp.int32(0)
    top = jnp.full((row_total,), MASKED, jnp.float32)
    total = jnp.zeros((row_total,), jnp.float32)
    summed = jnp.zeros((row_total, value_width), jnp.float32)
    keys = lax.all_gather(comp_keys, "seq", axis=0, tiled=True)
    values = lax.all_gather(comp_values, "seq", axis=0, tiled=True)
    length = keys.shape[0]
    block = length
    for size in (1024, 512, 256, 128):
        if length % size == 0:
            block = size
            break
    for index in range(length // block):
        key_block = keys[index * block : (index + 1) * block]
        value_block = values[index * block : (index + 1) * block]
        scores = (
            jnp.einsum("rd,kd->rk", rows, key_block, preferred_element_type=jnp.float32) * scale
        )
        key_at = start + index * block + jnp.arange(block, dtype=jnp.int32)
        scores = jnp.where(key_at[None, :] > 0, scores, MASKED)
        newtop = jnp.maximum(top, jnp.max(scores, axis=1))
        factor = jnp.exp(top - newtop)
        weights = jnp.exp(scores - newtop[:, None])
        total = total * factor + jnp.sum(weights, axis=1)
        summed = summed * factor[:, None] + jnp.dot(
            weights.astype(jnp.bfloat16), value_block, preferred_element_type=jnp.float32
        )
        top = newtop
    top, total, summed = (top, total, summed)
    compressed_out = summed / total[:, None]
    chosen = select_blocks.reshape(-1)
    shard_blocks = cache_count // SEL_BLOCK
    capacity = max(2, 2 * chosen.shape[0] // ranks)
    owner = chosen // shard_blocks
    local = chosen - owner * shard_blocks
    onehot = (owner[:, None] == jnp.arange(ranks, dtype=jnp.int32)[None, :]).astype(jnp.int32)
    position = jnp.sum((jnp.cumsum(onehot, axis=0) - 1) * onehot, axis=1)
    request = jnp.full((ranks, capacity), -1, jnp.int32).at[owner, position].set(local)
    key_blocks = cache_keys.reshape(shard_blocks, SEL_BLOCK, key_width)
    value_block_list = cache_values.reshape(shard_blocks, SEL_BLOCK, value_width)
    safe = jnp.clip(
        lax.all_to_all(request, "seq", split_axis=0, concat_axis=0, tiled=True), 0, shard_blocks - 1
    )
    got_keys = lax.all_to_all(key_blocks[safe], "seq", split_axis=0, concat_axis=0, tiled=True)
    got_values = lax.all_to_all(
        value_block_list[safe], "seq", split_axis=0, concat_axis=0, tiled=True
    )
    where_at = owner * capacity + position
    tile_count = select_blocks.shape[0]
    gathered_keys = got_keys.reshape(ranks * capacity, SEL_BLOCK, key_width)[where_at]
    picked_values = got_values.reshape(ranks * capacity, SEL_BLOCK, value_width)[where_at]
    gathered_keys, picked_values = (
        gathered_keys.reshape(tile_count, -1, key_width),
        picked_values.reshape(tile_count, -1, value_width),
    )
    tile_count = gathered_keys.shape[0]
    tile_row_count = rows.reshape(tile_count, -1, key_width)
    tile_scores = (
        jnp.einsum(
            "izu,ixu->izx", tile_row_count, gathered_keys, preferred_element_type=jnp.float32
        )
        * scale
    )
    selected_out = finish_rows(tile_scores, picked_values).reshape(row_total, value_width)
    context_keys = jnp.concatenate(near_keys)
    context_values = jnp.concatenate(near_values)
    context_positions = jnp.concatenate(nearby_positions)
    context_valid = jnp.concatenate(near_valid)
    sliding_scores = (
        jnp.einsum("rd,kd->rk", rows, context_keys, preferred_element_type=jnp.float32) * scale
    )
    allowed = (
        context_valid[None, :]
        & (context_positions[None, :] <= stretch_pos[:, None])
        & (context_positions[None, :] > stretch_pos[:, None] - WINDOW)
    )
    sliding_scores = jnp.where(
        allowed[:, None, :], sliding_scores.reshape(query_count, heads, -1), MASKED
    )
    window_out = finish_rows(sliding_scores.reshape(row_total, -1), context_values)
    logits = jnp.einsum(
        "thd,hdb->thb",
        queries.reshape(query_count, heads, key_width),
        gate_weight,
        preferred_element_type=jnp.float32,
    )
    gates = jax.nn.sigmoid(logits)
    mixed = (
        gates[:, :, 0:1] * compressed_out.reshape(query_count, heads, value_width)
        + gates[:, :, 1:2] * selected_out.reshape(query_count, heads, value_width)
        + gates[:, :, 2:3] * window_out.reshape(query_count, heads, value_width)
    )
    return mixed.astype(jnp.bfloat16).reshape(query_count, heads * value_width)


def solution(mesh):
    placed = (
        P("seq", "kv"),
        P("seq", "kv"),
        P("seq", "kv"),
        P("seq", "kv"),
        P("seq", "kv"),
        P("kv", None),
        P("kv", None),
        P("seq", "kv", None),
        P("kv", None, None),
    )
    return jax.shard_map(
        shards, mesh=mesh, in_specs=placed, out_specs=P("seq", "kv"), check_vma=False
    )
```

profile of v0, /device:TPU:1, one launch (start us, length us, event | category | flops | bytes accessed | tf_op | source)
XLA Modules:
  0.0 310.2 jit_solution(10423262976556319975)
XLA Ops:
  10.3 2.7 collective-permute-start
  16.7 10.2 %scatter_fusion = s32[8,16]{1,0:T(8,128)} fusion(s32[8,16]{1,0:T(8,128)} %broadcast_in_dim.83, s32[64]{0:T(128)S(1)} %fusion.59, s32[64]{0:T(128)S(1)} %get-tuple-element.7), kind=kCustom, calls=%fused_computation.4 | custom fusion | bytes 1280 | tf_op jit(solution)/shard_map/scatter | solution.py:164
  26.9 4.1 %all-to-all-start = ((s32[8,1,16]{2,1,0:T(1,128)}), s32[8,1,16]{2,1,0:T(1,128)}, u32[]{:S(2)}, u32[]{:S(2)}) async-start(s32[8,1,16]{2,1,0:T(1,128)} %bitcast.10), calls=%async_computation | async-start | bytes 8192 | tf_op jit(solution)/shard_map/all_to_all | solution.py:168
  32.0 2.1 reshape.394
  34.2 2.1 reshape_reshape.6
  43.5 2.5 copy.51
  47.3 1.4 copy.36
  50.9 2.8 gather_fusion
  53.7 2.2 gather_fusion.2
  55.9 5.1 %all-to-all-start.2 = ((bf16[8,16,64,128]{3,2,1,0:T(8,128)(2,1)}), bf16[8,16,64,128]{3,2,1,0:T(8,128)(2,1)}, u32[]{:S(2)}, u32[]{:S(2)}) async-start(bf16[8,16,64,128]{3,2,1,0:T(8,128)(2,1)} %bitcast.113), calls=%async_computation.2 | async-start | bytes 4194304 | tf_op jit(solution)/shard_map/all_to_all | solution.py:171
  61.8 4.9 %collective-permute-start.1 = (bf16[204800]{0:T(1024)(128)(2,1)}, bf16[204800]{0:T(1024)(128)(2,1)}, u32[]{:S(2)}, u32[]{:S(2)}) collective-permute-start(bf16[204800]{0:T(1024)(128)(2,1)} %pad_maximum_fusion), channel_id=1, source_target_pairs={{0,4},{1,5},{2,6},{3,7},{8,12},{9,13},{10,14},{11,15},{16,20},{17,... | collective-permute-start | bytes 1228808 | tf_op jit(solution)/shard_map/ppermute | solution.py:23
  66.8 2.0 collective-permute-start.2
  68.8 3.7 %collective-permute-start.3 = (bf16[204800]{0:T(1024)(128)(2,1)}, bf16[204800]{0:T(1024)(128)(2,1)}, u32[]{:S(2)}, u32[]{:S(2)}) collective-permute-start(bf16[204800]{0:T(1024)(128)(2,1)} %pad_maximum_fusion), channel_id=1, source_target_pairs={{0,2},{1,3},{2,4},{3,5},{4,6},{5,7},{8,10},{9,11},{10,12},{11,13},... | collective-permute-start | bytes 1228808 | tf_op jit(solution)/shard_map/ppermute | solution.py:23
  72.5 2.1 collective-permute-start.4
  80.8 23.3 %collective-permute-done.1 = bf16[204800]{0:T(1024)(128)(2,1)} collective-permute-done((bf16[204800]{0:T(1024)(128)(2,1)}, bf16[204800]{0:T(1024)(128)(2,1)}, u32[]{:S(2)}, u32[]{:S(2)}) %collective-permute-start.1) | collective-permute-done | bytes 409632 | tf_op jit(solution)/shard_map/ppermute | solution.py:23
  105.5 7.4 %collective-permute-done.2 = bf16[204800]{0:T(1024)(128)(2,1)} collective-permute-done((bf16[204800]{0:T(1024)(128)(2,1)}, bf16[204800]{0:T(1024)(128)(2,1)}, u32[]{:S(2)}, u32[]{:S(2)}) %collective-permute-start.2) | collective-permute-done | bytes 409632 | tf_op jit(solution)/shard_map/ppermute | solution.py:23
  114.3 7.4 %collective-permute-done.3 = bf16[204800]{0:T(1024)(128)(2,1)} collective-permute-done((bf16[204800]{0:T(1024)(128)(2,1)}, bf16[204800]{0:T(1024)(128)(2,1)}, u32[]{:S(2)}, u32[]{:S(2)}) %collective-permute-start.3) | collective-permute-done | bytes 409632 | tf_op jit(solution)/shard_map/ppermute | solution.py:23
  121.7 4.6 %collective-permute-done.4 = bf16[204800]{0:T(1024)(128)(2,1)} collective-permute-done((bf16[204800]{0:T(1024)(128)(2,1)}, bf16[204800]{0:T(1024)(128)(2,1)}, u32[]{:S(2)}, u32[]{:S(2)}) %collective-permute-start.4) | collective-permute-done | bytes 409632 | tf_op jit(solution)/shard_map/ppermute | solution.py:23
  134.2 29.5 %all-to-all-start.1 = ((bf16[8,16,64,192]{3,2,1,0:T(8,128)(2,1)}), bf16[8,16,64,192]{3,2,1,0:T(8,128)(2,1)}, u32[]{:S(2)}, u32[]{:S(2)}) async-start(bf16[8,16,64,192]{3,2,1,0:T(8,128)(2,1)} %bitcast.110), calls=%async_computation.1 | async-start | bytes 8388608 | tf_op jit(solution)/shard_map/all_to_all | solution.py:170
  165.9 3.2 %fusion.65 = (f32[2048]{0:T(1024)S(1)}, f32[2048,1152]{0,1:T(8,128)S(1)}) fusion(pred[2048,1152]{0,1:T(32,128)(4,1)S(1)} %copy.51, bf16[1152,192]{1,0:T(8,128)(2,1)S(1)} %constant_dynamic-update-slice_fusion.1, bf16[2048,192]{1,0:T(8,128)(2,1)} %reshape.394), kind=kOutput, calls=%fused_computation.126 | convolution fusion | flops 913045504 | bytes 13033472 | tf_op jit(solution)/shard_map/rd,kd->rk/dot_general | solution.py:196
  170.4 1.8 fusion.16
  176.0 88.0 %all_gather.15 = bf16[512,128]{1,0:T(8,128)(2,1)S(1)} all-gather(bf16[64,128]{1,0:T(8,128)(2,1)S(1)} %fusion.37), channel_id=1, replica_groups=mesh['kv'=4,'seq'=8] {'seq'}, dimensions={0}, use_global_device_ids=true | all-gather | bytes 147456 | tf_op jit(solution)/shard_map/all_gather | solution.py:132
  263.9 1.8 fusion.23
  265.7 1.9 fusion.30
  267.6 14.4 %all_gather.13 = bf16[512,192]{1,0:T(8,128)(2,1)S(1)} all-gather(bf16[64,192]{1,0:T(8,128)(2,1)S(1)} %fusion.30), channel_id=1, replica_groups=mesh['kv'=4,'seq'=8] {'seq'}, dimensions={0}, use_global_device_ids=true | all-gather | bytes 221184 | tf_op jit(solution)/shard_map/all_gather | solution.py:131
  283.9 1.5 fusion.15
  286.6 3.4 %gather_fusion.3 = bf16[64,64,128]{2,1,0:T(8,128)(2,1)} fusion(bf16[128,64,128]{2,1,0:T(8,128)(2,1)} %bitcast.20, s32[1024]{0:T(1024)} %pad_clamp_fusion), kind=kCustom, calls=%fused_computation.3 | custom fusion | bytes 2097408 | tf_op jit(solution)/shard_map/gather | solution.py:177
  290.0 3.0 gather_fusion.1
  294.3 1.4 fusion.3
  295.7 3.2 %fusion.41 = f32[4,512,128]{2,1,0:T(8,128)} fusion(bf16[4,1024,128]{2,1,0:T(8,128)(2,1)S(1)} %bitcast.119, f32[4,1024,512]{2,1,0:T(8,128)S(1)} %get-tuple-element.17, f32[4,512]{1,0:T(4,128)S(1)} %get-tuple-element.16, f32[4,512]{1,0:T(4,128)S(1)} %fusion.3), kind=kOutput, calls=%fused_computation.50 | convolution fusion | flops 543424512 | bytes 10502144 | tf_op jit(solution)/shard_map/dot_general | solution.py:40
  298.9 1.5 reshape_reshape.7
  301.4 1.9 fusion.39
  (153 shorter events, 49.0 us)
Async XLA Ops:
  6.5 25.3 %copy-start.6 = (bf16[1024,192]{0,1:T(8,128)(2,1)S(1)}, bf16[1024,192]{0,1:T(8,128)(2,1)}, u32[]{:S(2)}) copy-start(bf16[1024,192]{0,1:T(8,128)(2,1)} %param.10) | copy-start | bytes 1179652
  6.5 25.5 %copy-start.1 = (bf16[128,3072]{1,0:T(8,128)(2,1)S(1)}, bf16[128,3072]{1,0:T(8,128)(2,1)}, u32[]{:S(2)}) copy-start(bf16[128,3072]{1,0:T(8,128)(2,1)} %param.9) | copy-start | bytes 2359300
  6.5 166.9 %all-gather.5.cloned.1.call-start = ((), (), s32[]{:S(2)}) async-start(), calls=%async_computation.4 | async-start | bytes 1310720 | tf_op jit(solution)/shard_map/all_gather | solution.py:68
  10.3 28.9 %copy-start.18 = (bf16[16,192,3]{1,0,2:T(8,128)(2,1)S(1)}, bf16[16,192,3]{1,0,2:T(8,128)(2,1)}, u32[]{:S(2)}) copy-start(bf16[16,192,3]{1,0,2:T(8,128)(2,1)} %param.17) | copy-start | bytes 55300
  10.3 50.6 %collective-permute-start = (bf16[163840]{0:T(1024)(128)(2,1)}, bf16[163840]{0:T(1024)(128)(2,1)}, u32[]{:S(2)}, u32[]{:S(2)}) collective-permute-start(bf16[163840]{0:T(1024)(128)(2,1)} %pad_maximum_fusion.2), channel_id=1, source_target_pairs={{7,0},{0,1},{1,2},{2,3},{3,4},{4,5},{5,6},{6,7},{15,8},{8,9},{9,10... | collective-permute-start | bytes 983048 | tf_op jit(solution)/shard_map/ppermute | solution.py:17
  26.9 13.5 %copy-start = (bf16[1024,128]{1,0:T(8,128)(2,1)S(1)}, bf16[1024,128]{1,0:T(8,128)(2,1)}, u32[]{:S(2)}) copy-start(bf16[1024,128]{1,0:T(8,128)(2,1)} %param.11) | copy-start | bytes 786436
  26.9 23.3 %all-to-all-start = ((s32[8,1,16]{2,1,0:T(1,128)}), s32[8,1,16]{2,1,0:T(1,128)}, u32[]{:S(2)}, u32[]{:S(2)}) async-start(s32[8,1,16]{2,1,0:T(1,128)} %bitcast.10), calls=%async_computation | async-start | bytes 8192 | tf_op jit(solution)/shard_map/all_to_all | solution.py:168
  31.0 232.9 %all-gather.3.cloned.1.call-start = ((), (), s32[]{:S(2)}) async-start(), calls=%async_computation.3 | async-start | bytes 2949120 | tf_op jit(solution)/shard_map/all_gather | solution.py:67
  31.7 10.3 %copy-start.17 = (bf16[128,192]{0,1:T(8,128)(2,1)S(1)}, bf16[128,192]{0,1:T(8,128)(2,1)}, u32[]{:S(2)}) copy-start(bf16[128,192]{0,1:T(8,128)(2,1)} %param.12) | copy-start | bytes 147460
  42.1 1.4 copy-start.9
  53.7 7.3 %copy-start.15 = (bf16[24576]{0:T(1024)(128)(2,1)S(1)}, bf16[24576]{0:T(1024)(128)(2,1)}, u32[]{:S(2)}) copy-start(bf16[24576]{0:T(1024)(128)(2,1)} %reshape.406) | copy-start | bytes 147460
  53.7 7.3 %copy-start.16 = (bf16[128,128]{1,0:T(8,128)(2,1)S(1)}, bf16[128,128]{1,0:T(8,128)(2,1)}, u32[]{:S(2)}) copy-start(bf16[128,128]{1,0:T(8,128)(2,1)} %param.13) | copy-start | bytes 98308
  55.9 78.3 %all-to-all-start.2 = ((bf16[8,16,64,128]{3,2,1,0:T(8,128)(2,1)}), bf16[8,16,64,128]{3,2,1,0:T(8,128)(2,1)}, u32[]{:S(2)}, u32[]{:S(2)}) async-start(bf16[8,16,64,128]{3,2,1,0:T(8,128)(2,1)} %bitcast.113), calls=%async_computation.2 | async-start | bytes 4194304 | tf_op jit(solution)/shard_map/all_to_all | solution.py:171
  61.8 42.3 %collective-permute-start.1 = (bf16[204800]{0:T(1024)(128)(2,1)}, bf16[204800]{0:T(1024)(128)(2,1)}, u32[]{:S(2)}, u32[]{:S(2)}) collective-permute-start(bf16[204800]{0:T(1024)(128)(2,1)} %pad_maximum_fusion), channel_id=1, source_target_pairs={{0,4},{1,5},{2,6},{3,7},{8,12},{9,13},{10,14},{11,15},{16,20},{17,... | collective-permute-start | bytes 1228808 | tf_op jit(solution)/shard_map/ppermute | solution.py:23
  66.8 46.2 %collective-permute-start.2 = (bf16[204800]{0:T(1024)(128)(2,1)}, bf16[204800]{0:T(1024)(128)(2,1)}, u32[]{:S(2)}, u32[]{:S(2)}) collective-permute-start(bf16[204800]{0:T(1024)(128)(2,1)} %pad_maximum_fusion), channel_id=1, source_target_pairs={{0,3},{1,4},{2,5},{3,6},{4,7},{8,11},{9,12},{10,13},{11,14},{12,15... | collective-permute-start | bytes 1228808 | tf_op jit(solution)/shard_map/ppermute | solution.py:23
  68.8 52.9 %collective-permute-start.3 = (bf16[204800]{0:T(1024)(128)(2,1)}, bf16[204800]{0:T(1024)(128)(2,1)}, u32[]{:S(2)}, u32[]{:S(2)}) collective-permute-start(bf16[204800]{0:T(1024)(128)(2,1)} %pad_maximum_fusion), channel_id=1, source_target_pairs={{0,2},{1,3},{2,4},{3,5},{4,6},{5,7},{8,10},{9,11},{10,12},{11,13},... | collective-permute-start | bytes 1228808 | tf_op jit(solution)/shard_map/ppermute | solution.py:23
  72.5 53.8 %collective-permute-start.4 = (bf16[204800]{0:T(1024)(128)(2,1)}, bf16[204800]{0:T(1024)(128)(2,1)}, u32[]{:S(2)}, u32[]{:S(2)}) collective-permute-start(bf16[204800]{0:T(1024)(128)(2,1)} %pad_maximum_fusion), channel_id=1, source_target_pairs={{0,1},{1,2},{2,3},{3,4},{4,5},{5,6},{6,7},{8,9},{9,10},{10,11},{11... | collective-permute-start | bytes 1228808 | tf_op jit(solution)/shard_map/ppermute | solution.py:23
  134.2 31.6 %copy-start.10 = (bf16[128,192]{1,0:T(8,128)(2,1)S(1)}, bf16[128,192]{1,0:T(8,128)(2,1)}, u32[]{:S(2)}) copy-start(bf16[128,192]{1,0:T(8,128)(2,1)} %copy-done.9) | copy-start | bytes 147460
  134.2 155.8 %all-to-all-start.1 = ((bf16[8,16,64,192]{3,2,1,0:T(8,128)(2,1)}), bf16[8,16,64,192]{3,2,1,0:T(8,128)(2,1)}, u32[]{:S(2)}, u32[]{:S(2)}) async-start(bf16[8,16,64,192]{3,2,1,0:T(8,128)(2,1)} %bitcast.110), calls=%async_computation.1 | async-start | bytes 8388608 | tf_op jit(solution)/shard_map/all_to_all | solution.py:170
  169.1 1.4 copy-start.19
  170.4 4.3 %copy-start.8 = (bf16[64,2048]{1,0:T(8,128)(2,1)S(1)}, bf16[64,2048]{1,0:T(8,128)(2,1)}, u32[]{:S(2)}) copy-start(bf16[64,2048]{1,0:T(8,128)(2,1)} %reshape.396) | copy-start | bytes 786436
  170.4 93.5 %copy-start.11 = (bf16[64,3072]{1,0:T(8,128)(2,1)S(1)}, bf16[64,3072]{1,0:T(8,128)(2,1)}, u32[]{:S(2)}) copy-start(bf16[64,3072]{1,0:T(8,128)(2,1)} %reshape.393) | copy-start | bytes 1179652
  172.3 109.8 %copy-start.3 = (bf16[2048,192]{1,0:T(8,128)(2,1)S(1)}, bf16[2048,192]{1,0:T(8,128)(2,1)}, u32[]{:S(2)}) copy-start(bf16[2048,192]{1,0:T(8,128)(2,1)} %reshape.394) | copy-start | bytes 2359300
  172.3 109.8 %copy-start.20 = (pred[512]{0:T(512)(128)(4,1)S(1)}, pred[512]{0:T(512)(128)(4,1)}, u32[]{:S(2)}) copy-start(pred[512]{0:T(512)(128)(4,1)} %iota_compare_fusion.1) | copy-start | bytes 1540
  285.4 7.6 %copy-start.2 = (bf16[4,512,192]{2,1,0:T(8,128)(2,1)S(1)}, bf16[4,512,192]{2,1,0:T(8,128)(2,1)}, u32[]{:S(2)}) copy-start(bf16[4,512,192]{2,1,0:T(8,128)(2,1)} %reshape_reshape.6) | copy-start | bytes 2359300
  294.3 1.4 copy-start.7
  295.7 4.7 %copy-start.12 = (f32[128,16]{1,0:T(8,128)S(1)}, f32[128,16]{1,0:T(8,128)}, u32[]{:S(2)}) copy-start(f32[128,16]{1,0:T(8,128)} %copy.36) | copy-start | bytes 24580
  295.7 5.1 %copy-start.13 = (f32[128,16]{1,0:T(8,128)S(1)}, f32[128,16]{1,0:T(8,128)}, u32[]{:S(2)}) copy-start(f32[128,16]{1,0:T(8,128)} %copy.41) | copy-start | bytes 24580
  298.8 2.2 copy-start.14
  298.8 2.6 copy-start.4
  298.8 2.6 copy-start.5
Sparse Core Ops, SparseCore 0:
  9.2 28.4 all-gather.4
  39.5 37.3 all-gather.2
where the time goes:
time: 312 us; the launch traced here: 310 us
  blocking collectives  102 us (33%)
  local copies, waits for them, and re-layouts  62.7 us (20%)
  starting transfers between devices  54.2 us (17%)
  waiting for transfers between devices  44.2 us (14%)
  matrix products  18.3 us (6%)
  other arithmetic  14.3 us (5%)
  between operations  14 us (4%)
    all_gather x1, blocking collectives, shards(): values = lax.all_gather(comp_values, 'seq', axis=0, tiled=True)  88 us
    ppermute x4, waiting for transfers between devices, from_behind(): return lax.ppermute(x, axis, pairs)  42.7 us
    all_to_all x1, starting transfers between devices, shards(): lax.all_to_all(key_blocks[safe], 'seq', split_axis=0, concat_axis=0, tile...  29.5 us
    all_gather x1, blocking collectives, shards(): keys = lax.all_gather(comp_keys, 'seq', axis=0, tiled=True)  14.4 us
    ppermute x4, starting transfers between devices, from_behind(): return lax.ppermute(x, axis, pairs)  12.8 us
    scatter x1, local copies, waits for them, and re-layouts, shards(): jnp.full((ranks, capacity), -1, jnp.int32).at[owner, position].set(local)  10.2 us
    unnamed x61, local copies, waits for them, and re-layouts  8.66 us
  transfers between devices with their start and end apart: 10, of which 4 were waited for; matrix products, arithmetic and copies ran while one was open for 26% of the time, Pallas kernels for 0%

commit v1 on v0

--- a/solution.py
+++ b/solution.py
@@ -1,6 +1,10 @@
+import functools
+
 import jax
 import jax.numpy as jnp
 from jax import lax
+from jax.experimental import pallas as pl
+from jax.experimental.pallas import tpu as pltpu
 from jax.sharding import PartitionSpec as P
 
 CMP_STRIDE = 16
@@ -41,7 +45,7 @@
     return mixed / total
 
 
-def shards(
+def shards_by_request(
     queries,
     cache_keys,
     cache_values,
@@ -219,6 +223,606 @@
     return mixed.astype(jnp.bfloat16).reshape(query_count, heads * value_width)
 
 
+CORES = 2
+LOG2E = 1.4426950408889634
+MESH = pl.DeviceIdType.MESH
+
+
+def gather_kernel(
+    n_seq,
+    n_kv,
+    hops,
+    ck,
+    cv,
+    klo,
+    ik,
+    iv,
+    iklo,
+    wk,
+    wv,
+    ckr,
+    cvr,
+    kh_out,
+    v_out,
+    kl_out,
+    nkh_out,
+    nv_out,
+    nkl_out,
+    compk_out,
+    compv_out,
+    ck_vm,
+    cv_vm,
+    klo_vm,
+    ik_vm,
+    iv_vm,
+    iklo_vm,
+    lhs_k,
+    lhs_v,
+    wk_all,
+    wv_all,
+    compk_vm,
+    compv_vm,
+    local_sem,
+    own_sem,
+    kv_send,
+    kv_recv,
+    new_send,
+    new_recv,
+    edge_send,
+    edge_recv,
+    w_send,
+    w_recv,
+    comp_send,
+    comp_recv,
+):
+    me = lax.axis_index("seq")
+    group = lax.axis_index("kv")
+    z = me // CORES
+    core = lax.rem(me, CORES)
+    chips = n_seq // CORES
+    mate = z * CORES + 1 - core
+    left = lax.rem(me - CORES + n_seq, n_seq)
+    right = lax.rem(me + CORES, n_seq)
+    width_v = cv.shape[1]
+    rows = ckr.shape[0]
+
+    barrier = pltpu.get_barrier_semaphore()
+    for d in range(1, n_seq):
+        pl.semaphore_signal(
+            barrier, inc=1, device_id={"seq": lax.rem(me + d, n_seq)}, device_id_type=MESH
+        )
+    for d in range(1, n_kv):
+        pl.semaphore_signal(
+            barrier, inc=1, device_id={"kv": lax.rem(group + d, n_kv)}, device_id_type=MESH
+        )
+
+    loads = [
+        (ck, ck_vm),
+        (cv, cv_vm),
+        (klo, klo_vm),
+        (ik, ik_vm),
+        (iv, iv_vm),
+        (iklo, iklo_vm),
+        (ckr, lhs_k.at[pl.ds(16, rows)]),
+        (cvr, lhs_v.at[pl.ds(16, rows)]),
+    ]
+    half_k = wk.shape[0] // CORES
+    half_v = wv.shape[0] // CORES
+    for half in range(CORES):
+        loads.append((wk.at[pl.ds(half * half_k, half_k)], wk_all.at[group, half]))
+        loads.append((wv.at[pl.ds(half * half_v, half_v)], wv_all.at[group, half]))
+    load_copies = [pltpu.make_async_copy(a, b, local_sem.at[n]) for n, (a, b) in enumerate(loads)]
+    for copy in load_copies:
+        copy.start()
+
+    pl.semaphore_wait(barrier, n_seq - 1 + n_kv - 1)
+
+    old_outs = (kh_out, v_out, kl_out)
+    new_outs = (nkh_out, nv_out, nkl_out)
+    old_own = (ck.at[:, pl.ds(0, width_v)], cv, klo)
+    new_own = (ik.at[:, pl.ds(0, width_v)], iv, iklo)
+    route = (left, right, mate)
+
+    def message(outs, own, sends, recvs, slot, way, part):
+        source = outs[part].at[slot] if own is None else own[part]
+        return pltpu.make_async_remote_copy(
+            src_ref=source,
+            dst_ref=outs[part].at[slot],
+            send_sem=sends.at[way, slot, part],
+            recv_sem=recvs.at[slot, part],
+            device_id={"seq": route[way]},
+            device_id_type=MESH,
+        )
+
+    def old_msg(slot, way, part, own=None):
+        return message(old_outs, own, kv_send, kv_recv, slot, way, part)
+
+    def new_msg(slot, way, part, own=None):
+        return message(new_outs, own, new_send, new_recv, slot, way, part)
+
+    PARTS = range(3)
+
+    def start(make, slot, way, own=None):
+        for part in PARTS:
+            make(slot, way, part, own).start()
+
+    def recv(make, slot):
+        for part in PARTS:
+            make(slot, 2, part).wait_recv()
+
+    def sent(make, slot, way, own=None):
+        for part in PARTS:
+            make(slot, way, part, own).wait_send()
+
+    @pl.when(z < chips - 1)
+    def _():
+        start(new_msg, me, 1, new_own)
+
+    start(new_msg, me, 2, new_own)
+
+    nxt = lax.rem(me + 1, n_seq)
+    prev = lax.rem(me + n_seq - 1, n_seq)
+    edges = [
+        pltpu.make_async_remote_copy(
+            src_ref=src.at[pl.ds(rows - 16, 16)],
+            dst_ref=dst.at[pl.ds(0, 16)],
+            send_sem=edge_send.at[n],
+            recv_sem=edge_recv.at[n],
+            device_id={"seq": nxt},
+            device_id_type=MESH,
+        )
+        for n, (src, dst) in enumerate(((ckr, lhs_k), (cvr, lhs_v)))
+    ]
+    for copy in edges:
+        copy.start()
+
+    @pl.when(z < chips - 1)
+    def _():
+        start(old_msg, me, 1, old_own)
+
+    @pl.when(z > 0)
+    def _():
+        start(old_msg, me, 0, old_own)
+
+    w_all = (wk_all, wv_all)
+    w_own = (
+        wk.at[pl.ds(pl.multiple_of(core * half_k, half_k), half_k)],
+        wv.at[pl.ds(pl.multiple_of(core * half_v, half_v), half_v)],
+    )
+
+    def w_msg(d, part):
+        return pltpu.make_async_remote_copy(
+            src_ref=w_own[part],
+            dst_ref=w_all[part].at[group, core],
+            send_sem=w_send.at[d - 1, part],
+            recv_sem=w_recv.at[group, core, part],
+            device_id={"kv": lax.rem(group + d, n_kv)},
+            device_id_type=MESH,
+        )
+
+    def w_arrived(who, half, part):
+        return pltpu.make_async_remote_copy(
+            src_ref=w_all[part].at[who, half],
+            dst_ref=w_all[part].at[who, half],
+            send_sem=w_send.at[n_kv - 1 + lax.rem(who - group + n_kv, n_kv) - 1, part],
+            recv_sem=w_recv.at[who, half, part],
+            device_id={"seq": mate},
+            device_id_type=MESH,
+        )
+
+    for d in range(1, n_kv):
+        for part in range(2):
+            w_msg(d, part).start()
+
+    start(old_msg, me, 2, old_own)
+
+    for copy in load_copies:
+        copy.wait()
+    keeps = [
+        (ck_vm.at[:, pl.ds(0, width_v)], kh_out.at[me]),
+        (cv_vm, v_out.at[me]),
+        (klo_vm, kl_out.at[me]),
+        (ik_vm.at[:, pl.ds(0, width_v)], nkh_out.at[me]),
+        (iv_vm, nv_out.at[me]),
+        (iklo_vm, nkl_out.at[me]),
+    ]
+    keep_copies = [pltpu.make_async_copy(a, b, own_sem.at[n]) for n, (a, b) in enumerate(keeps)]
+    for copy in keep_copies:
+        copy.start()
+
+    for d in range(1, min(hops, chips - 1) + 1):
+
+        @pl.when(z >= d)
+        def _():
+            slot = me - CORES * d
+            recv(new_msg, slot)
+            if d < hops:
+
+                @pl.when(z < chips - 1)
+                def _():
+                    start(new_msg, slot, 1)
+
+            start(new_msg, slot, 2)
+
+    def relay(d):
+        @pl.when(z >= d)
+        def _():
+            slot = me - CORES * d
+            recv(old_msg, slot)
+
+            @pl.when(z < chips - 1)
+            def _():
+                start(old_msg, slot, 1)
+
+            start(old_msg, slot, 2)
+
+        @pl.when(z + d < chips)
+        def _():
+            slot = me + CORES * d
+            recv(old_msg, slot)
+
+            @pl.when(z > 0)
+            def _():
+                start(old_msg, slot, 0)
+
+            start(old_msg, slot, 2)
+
+    comps = ((compk_vm, compk_out), (compv_vm, compv_out))
+
+    def comp_msg(d, part):
+        return pltpu.make_async_remote_copy(
+            src_ref=comps[part][0],
+            dst_ref=comps[part][1].at[me],
+            send_sem=comp_send.at[d - 1, part],
+            recv_sem=comp_recv.at[me, part],
+            device_id={"seq": lax.rem(me + d, n_seq)},
+            device_id_type=MESH,
+        )
+
+    def compress():
+        for d in range(1, n_kv):
+            who = lax.rem(group + n_kv - d, n_kv)
+            for part in range(2):
+                w_arrived(who, core, part).wait_recv()
+                w_arrived(who, core, part).start()
+        for d in range(1, n_kv):
+            who = lax.rem(group + n_kv - d, n_kv)
+            for part in range(2):
+                w_arrived(who, 1 - core, part).wait_recv()
+        for copy in edges:
+            copy.wait_recv()
+        for lhs, w, (held, _) in ((lhs_k, wk_all, comps[0]), (lhs_v, wv_all, comps[1])):
+            depth = w.shape[2]
+            chunks = n_kv * CORES
+            sums = []
+            for side in range(2):
+                total = None
+                for n in range(chunks // 2):
+                    at = side * (chunks // 2) + n
+                    term = jnp.dot(
+                        lhs[:, n * depth : (n + 1) * depth],
+                        w[at // CORES, at % CORES],
+                        preferred_element_type=jnp.float32,
+                    )
+                    total = term if total is None else total + term
+                sums.append(total)
+            held[...] = (sums[0][15 : 15 + rows] + sums[1][16 : 16 + rows]).astype(jnp.bfloat16)
+        for d in range(1, n_seq):
+            for part in range(2):
+                comp_msg(d, part).start()
+        for part in range(2):
+            pltpu.make_async_copy(comps[part][0], comps[part][1].at[me], own_sem.at[6 + part]).start()
+
+    relay(1)
+    compress()
+    for d in range(2, chips):
+        relay(d)
+
+    for copy in keep_copies:
+        copy.wait()
+    for part in range(2):
+        pltpu.make_async_copy(comps[part][0], comps[part][1].at[me], own_sem.at[6 + part]).wait()
+    for zz in range(chips):
+        recv(old_msg, zz * CORES + 1 - core)
+    for d in range(0, min(hops, chips - 1) + 1):
+
+        @pl.when(z >= d)
+        def _():
+            recv(new_msg, (z - d) * CORES + 1 - core)
+
+    for d in range(1, n_seq):
+        who = lax.rem(me + d, n_seq)
+        for part in range(2):
+            pltpu.make_async_remote_copy(
+                src_ref=comps[part][0],
+                dst_ref=comps[part][1].at[who],
+                send_sem=comp_send.at[d - 1, part],
+                recv_sem=comp_recv.at[who, part],
+                device_id={"seq": who},
+                device_id_type=MESH,
+            ).wait_recv()
+    for copy in edges:
+        copy.wait_send()
+    for d in range(1, n_kv):
+        for part in range(2):
+            w_msg(d, part).wait_send()
+            w_arrived(lax.rem(group + n_kv - d, n_kv), core, part).wait_send()
+    for d in range(1, n_seq):
+        for part in range(2):
+            comp_msg(d, part).wait_send()
+
+    @pl.when(z < chips - 1)
+    def _():
+        sent(new_msg, me, 1, new_own)
+        sent(old_msg, me, 1, old_own)
+
+    @pl.when(z > 0)
+    def _():
+        sent(old_msg, me, 0, old_own)
+
+    sent(new_msg, me, 2, new_own)
+    sent(old_msg, me, 2, old_own)
+    for d in range(1, chips):
+
+        @pl.when(z >= d)
+        def _():
+            slot = me - CORES * d
+            if d <= hops:
+                sent(new_msg, slot, 2)
+
+                if d < hops:
+
+                    @pl.when(z < chips - 1)
+                    def _():
+                        sent(new_msg, slot, 1)
+
+            sent(old_msg, slot, 2)
+
+            @pl.when(z < chips - 1)
+            def _():
+                sent(old_msg, slot, 1)
+
+        @pl.when(z + d < chips)
+        def _():
+            slot = me + CORES * d
+            sent(old_msg, slot, 2)
+
+            @pl.when(z > 0)
+            def _():
+                sent(old_msg, slot, 0)
+
+
+def attend_kernel(
+    heads,
+    tile,
+    lookback,
+    sel,
+    q,
+    kh,
+    v,
+    kl,
+    nkh,
+    nv,
+    nkl,
+    compk,
+    compv,
+    gw,
+    out,
+    rows_vm,
+    win_k,
+    win_v,
+    sel_k,
+    sel_v,
+):
+    me = lax.axis_index("seq")
+    step = pl.program_id(0)
+    width = gw.shape[0]
+    vw = v.shape[2]
+    low = width - vw
+    factor = width**-0.5 * LOG2E
+    per = nkh.shape[1]
+    blocks_per = per // SEL_BLOCK
+
+    def put(dk, dv, at, khv, vv, klv):
+        half = SEL_BLOCK // 2
+        dk[pl.ds(at, SEL_BLOCK), 0:vw] = khv
+        dk[pl.ds(at, half), vw:width] = klv[:, 0:low]
+        dk[pl.ds(at + half, half), vw:width] = klv[:, low : 2 * low]
+        dv[pl.ds(at, SEL_BLOCK), :] = vv
+
+    @pl.when(step == 0)
+    def _():
+        total = kh.shape[0]
+        for i in range(lookback + 1):
+            chunk = me + i
+            for b in range(blocks_per):
+                at = i * per + b * SEL_BLOCK
+
+                @pl.when(chunk < lookback)
+                def _():
+                    block = total - lookback * blocks_per + chunk * blocks_per + b
+                    put(win_k, win_v, at, kh[block], v[block], kl[block])
+
+                @pl.when(chunk >= lookback)
+                def _():
+                    slot = chunk - lookback
+                    put(
+                        win_k,
+                        win_v,
+                        at,
+                        nkh[slot, b * SEL_BLOCK : (b + 1) * SEL_BLOCK],
+                        nv[slot, b * SEL_BLOCK : (b + 1) * SEL_BLOCK],
+                        nkl[slot, b * SEL_BLOCK // 2 : (b + 1) * SEL_BLOCK // 2],
+                    )
+
+    for h in range(heads):
+        rows_vm[h * tile : (h + 1) * tile, :] = q[:, h * width : (h + 1) * width]
+    picks = sel.shape[1]
+    for n in range(picks):
+        block = sel[step, n]
+        put(sel_k, sel_v, n * SEL_BLOCK, kh[block], v[block], kl[block])
+
+    logits = jnp.dot(rows_vm[...], gw[...], preferred_element_type=jnp.float32)
+    gates = jax.nn.sigmoid(logits)
+    span = WINDOW + tile
+    off = pl.multiple_of(step * tile, tile)
+
+    def attend(rows, keys, values, allowed):
+        s = lax.dot_general(
+            rows, keys, (((1,), (1,)), ((), ())), preferred_element_type=jnp.float32
+        )
+        if allowed is not None:
+            s = jnp.where(allowed, s, MASKED)
+        top = jnp.max(s, axis=-1, keepdims=True)
+        w = jnp.exp2((s - top) * factor)
+        total = jnp.sum(w, axis=-1, keepdims=True)
+        o = jnp.dot(w.astype(jnp.bfloat16), values, preferred_element_type=jnp.float32)
+        return o / total
+
+    group_heads = 4
+    count = group_heads * tile
+    comp_n = compk.shape[0]
+    comp_ok = lax.broadcasted_iota(jnp.int32, (count, comp_n), 1) > 0
+    diff = lax.broadcasted_iota(jnp.int32, (count, span), 1) - lax.rem(
+        lax.broadcasted_iota(jnp.int32, (count, span), 0), tile
+    )
+    win_ok = (diff > 0) & (diff <= WINDOW)
+    for g in range(heads // group_heads):
+        rows = rows_vm[g * count : (g + 1) * count, :]
+        c = attend(rows, compk[...], compv[...], comp_ok)
+        s = attend(rows, sel_k[...], sel_v[...], None)
+        w = attend(rows, win_k[pl.ds(off, span), :], win_v[pl.ds(off, span), :], win_ok)
+        for i in range(group_heads):
+            h = g * group_heads + i
+            a = slice(i * tile, (i + 1) * tile)
+            b = slice(h * tile, (h + 1) * tile)
+            mixed = (
+                gates[b, 3 * h : 3 * h + 1] * c[a]
+                + gates[b, 3 * h + 1 : 3 * h + 2] * s[a]
+                + gates[b, 3 * h + 2 : 3 * h + 3] * w[a]
+            )
+            out[:, h * vw : (h + 1) * vw] = mixed.astype(out.dtype)
+
+
+def pack_low(keys, vw):
+    low = keys.shape[1] - vw
+    part = keys[:, vw:].reshape(-1, 2, SEL_BLOCK // 2, low)
+    return jnp.concatenate([part[:, 0], part[:, 1]], axis=-1).reshape(-1, 2 * low)
+
+
+def shards_gathered(q, ck, cv, ik, iv, wk, wv, sel, gw):
+    n_seq, n_kv = lax.axis_size("seq"), lax.axis_size("kv")
+    heads, width, branches = gw.shape
+    vw = cv.shape[1]
+    cache, fresh = ck.shape[0], ik.shape[0]
+    tiles = sel.shape[0]
+    tile = fresh // tiles
+    lookback = WINDOW // fresh
+    hops = -(-lookback // CORES)
+    rows = cache // CMP_STRIDE
+    bf = jnp.bfloat16
+    any_spec = pl.BlockSpec(memory_space=pl.ANY)
+    half_k, half_v = wk.shape[0] // CORES, wv.shape[0] // CORES
+    gathered = pl.pallas_call(
+        functools.partial(gather_kernel, n_seq, n_kv, hops),
+        out_shape=[
+            jax.ShapeDtypeStruct((n_seq, cache, vw), bf),
+            jax.ShapeDtypeStruct((n_seq, cache, vw), bf),
+            jax.ShapeDtypeStruct((n_seq, cache // 2, vw), bf),
+            jax.ShapeDtypeStruct((n_seq, fresh, vw), bf),
+            jax.ShapeDtypeStruct((n_seq, fresh, vw), bf),
+            jax.ShapeDtypeStruct((n_seq, fresh // 2, vw), bf),
+            jax.ShapeDtypeStruct((n_seq, rows, width), bf),
+            jax.ShapeDtypeStruct((n_seq, rows, vw), bf),
+        ],
+        in_specs=[any_spec] * 10,
+        out_specs=[any_spec] * 8,
+        scratch_shapes=[
+            pltpu.VMEM((cache, width), bf),
+            pltpu.VMEM((cache, vw), bf),
+            pltpu.VMEM((cache // 2, vw), bf),
+            pltpu.VMEM((fresh, width), bf),
+            pltpu.VMEM((fresh, vw), bf),
+            pltpu.VMEM((fresh // 2, vw), bf),
+            pltpu.VMEM((rows + 16, CMP_STRIDE * width), bf),
+            pltpu.VMEM((rows + 16, CMP_STRIDE * vw), bf),
+            pltpu.VMEM((n_kv, CORES, half_k, width), bf),
+            pltpu.VMEM((n_kv, CORES, half_v, vw), bf),
+            pltpu.VMEM((rows, width), bf),
+            pltpu.VMEM((rows, vw), bf),
+            pltpu.SemaphoreType.DMA((12,)),
+            pltpu.SemaphoreType.DMA((8,)),
+            pltpu.SemaphoreType.DMA((3, n_seq, 3)),
+            pltpu.SemaphoreType.DMA((n_seq, 3)),
+            pltpu.SemaphoreType.DMA((3, n_seq, 3)),
+            pltpu.SemaphoreType.DMA((n_seq, 3)),
+            pltpu.SemaphoreType.DMA((2,)),
+            pltpu.SemaphoreType.DMA((2,)),
+            pltpu.SemaphoreType.DMA((2 * (n_kv - 1), 2)),
+            pltpu.SemaphoreType.DMA((n_kv, CORES, 2)),
+            pltpu.SemaphoreType.DMA((n_seq - 1, 2)),
+            pltpu.SemaphoreType.DMA((n_seq, 2)),
+        ],
+        compiler_params=pltpu.CompilerParams(collective_id=0, has_side_effects=True),
+    )(
+        ck,
+        cv,
+        pack_low(ck, vw),
+        ik,
+        iv,
+        pack_low(ik, vw),
+        wk,
+        wv,
+        ck.reshape(rows, CMP_STRIDE * width),
+        cv.reshape(rows, CMP_STRIDE * vw),
+    )
+    kh, v, kl, nkh, nv, nkl, compk, compv = gathered
+    blocks = n_seq * cache // SEL_BLOCK
+    kh = kh.reshape(blocks, SEL_BLOCK, vw)
+    v = v.reshape(blocks, SEL_BLOCK, vw)
+    kl = kl.reshape(blocks, SEL_BLOCK // 2, vw)
+    compk = compk.reshape(n_seq * rows, width)
+    compv = compv.reshape(n_seq * rows, vw)
+    gates = jnp.transpose(gw, (1, 0, 2)).reshape(width, heads * branches)
+
+    def whole(x):
+        return pl.BlockSpec(
+            x.shape, lambda i, s: (0,) * x.ndim, pipeline_mode=pl.Buffered(1)
+        )
+
+    fixed = [kh, v, kl, nkh, nv, nkl, compk, compv, gates]
+    picks = sel.shape[-1]
+    return pl.pallas_call(
+        functools.partial(attend_kernel, heads, tile, lookback),
+        out_shape=jax.ShapeDtypeStruct((fresh, heads * vw), bf),
+        grid_spec=pltpu.PrefetchScalarGridSpec(
+            num_scalar_prefetch=1,
+            grid=(tiles,),
+            in_specs=[pl.BlockSpec((tile, heads * width), lambda i, s: (i, 0))]
+            + [whole(x) for x in fixed],
+            out_specs=pl.BlockSpec((tile, heads * vw), lambda i, s: (i, 0)),
+            scratch_shapes=[
+                pltpu.VMEM((heads * tile, width), bf),
+                pltpu.VMEM((fresh + WINDOW, width), bf),
+                pltpu.VMEM((fresh + WINDOW, vw), bf),
+                pltpu.VMEM((picks * SEL_BLOCK, width), bf),
+                pltpu.VMEM((picks * SEL_BLOCK, vw), bf),
+            ],
+        ),
+        compiler_params=pltpu.CompilerParams(vmem_limit_bytes=60 << 20),
+    )(sel.reshape(tiles, picks), q, *fixed)
+
+
+GATHER_BYTES = 1 << 24
+
+
+def shards(queries, cache_keys, cache_values, *rest):
+    ranks = lax.axis_size("seq")
+    size = ranks * 2 * (cache_keys.size + cache_values.size)
+    form = shards_gathered if size <= GATHER_BYTES else shards_by_request
+    return form(queries, cache_keys, cache_values, *rest)
+
+
 def solution(mesh):
     placed = (
         P("seq", "kv"),

time: 312 us -> 99 us (0.32)
  blocking collectives: 102 us -> 0 us
  Pallas kernels: 0 us -> 91.7 us
  local copies, waits for them, and re-layouts: 62.7 us -> 5.52 us
  starting transfers between devices: 54.2 us -> 0 us
  waiting for transfers between devices: 44.2 us -> 0 us
  matrix products: 18.3 us -> 0 us
  between operations: 14 us -> 0.1 us
  other arithmetic: 14.3 us -> 1.43 us
    all_gather x2 -> x0, blocking collectives: 102 us -> none  [the longest x1 88 us: shards(): values = lax.all_gather(comp_values, 'seq', axis=0, tiled=True)]
    pallas_call x0 -> x2, Pallas kernels: none -> 91.7 us  [the longest x1 67.4 us: shards_gathered(): pl.pallas_call(functools.partial(gather_kernel, n_seq, n_kv, hops), out_s...]
    ppermute x5 -> x0, waiting for transfers between devices: 42.7 us -> none  [the longest x4 42.7 us: from_behind(): return lax.ppermute(x, axis, pairs)]
    all_to_all x3 -> x0, starting transfers between devices: 38.7 us -> none  [the longest x1 29.5 us: shards(): lax.all_to_all(key_blocks[safe], 'seq', split_axis=0, concat_axis=0, tile...]
    dot_general x11 -> x0, matrix products: 18.3 us -> none  [the longest x2 4.96 us: finish_rows(): jnp.matmul(weights.astype(jnp.bfloat16), values, preferred_element_type=j...]
    ppermute x5 -> x0, starting transfers between devices: 15.5 us -> none  [the longest x4 12.8 us: from_behind(): return lax.ppermute(x, axis, pairs)]
    gather x4 -> x0, local copies, waits for them, and re-layouts: 11.3 us -> none  [the longest x1 3.39 us: shards(): got_values.reshape(ranks * capacity, SEL_BLOCK, value_width)[where_at]]
    scatter x1 -> x0, local copies, waits for them, and re-layouts: 10.2 us -> none  [shards(): jnp.full((ranks, capacity), -1, jnp.int32).at[owner, position].set(local)]
  transfers between devices with their start and end apart: 10 -> 0, of which waited for: 4 -> 0; matrix products, arithmetic and copies ran while one was open for 26% -> 0% of each run, Pallas kernels for 0% -> 0%
where the time goes in v1:
time: 99 us; the launch traced here: 98.7 us
  Pallas kernels  91.7 us (93%)
  local copies, waits for them, and re-layouts  5.52 us (6%)
  other arithmetic  1.43 us (1%)
    pallas_call x1, Pallas kernels, shards_gathered(): pl.pallas_call(functools.partial(gather_kernel, n_seq, n_kv, hops), out_s...  67.4 us
    pallas_call x1, Pallas kernels, shards_gathered(): pl.pallas_call(functools.partial(attend_kernel, heads, tile, lookback), o...  24.2 us
    unnamed x15, local copies, waits for them, and re-layouts  2.58 us

profile of v1, /device:TPU:1, one launch (start us, length us, event | category | flops | bytes accessed | tf_op | source)
XLA Modules:
  0.0 98.7 jit_solution(520529745960275209)
XLA Ops:
  0.0 0.0 copy-start.4
  0.0 0.0 copy-start.2
  0.0 1.3 %copy.22.ck = bf16[1024,192]{1,0:T(8,128)(2,1)S(1)} copy(bf16[1024,192]{0,1:T(8,128)(2,1)} %param.10) | data formatting | bytes 786432 | tf_op args[1]
  1.3 0.0 copy-start
  1.3 0.0 copy-start.1
  1.3 0.8 pad_maximum_fusion.klo
  2.1 0.0 copy-done.4
  2.1 0.1 copy.23.ik
  2.2 0.0 copy-start.3
  2.3 0.7 pad_maximum_fusion.1.iklo
  2.9 1.3 %reshape.46.ckr = bf16[64,3072]{1,0:T(8,128)(2,1)} reshape(bf16[1024,192]{1,0:T(8,128)(2,1)S(1)} %copy.22.ck) | data formatting | bytes 786432 | tf_op jit(solution)/shard_map/reshape | solution.py:776
  4.2 0.0 copy-done.2
  4.2 0.0 copy-start.5
  4.2 1.2 %copy.24.wk = bf16[1536,192]{1,0:T(8,128)(2,1)} copy(bf16[1536,192]{0,1:T(8,128)(2,1)S(1)} %copy-done.2) | data formatting | bytes 1179648 | tf_op args[5]
  5.4 0.0 copy-done.1
  5.4 0.8 reshape.47.cvr
  6.3 0.0 copy-done
  6.3 0.0 copy-done.3
  6.3 67.4 %shard_map.91 = (bf16[8,1024,128]{2,1,0:T(8,128)(2,1)}, bf16[8,1024,128]{2,1,0:T(8,128)(2,1)}, bf16[8,512,128]{2,1,0:T(8,128)(2,1)}, bf16[8,128,128]{2,1,0:T(8,1...) custom-call(bf16[1024,192]{1,0:T(8,128)(2,1)} %copy-done, ...), custom_call_target="tpu_custom_call" | custom-call | tf_op jit(solution)/shard_map/pallas_call | solution.py:726
  73.7 0.0 copy-done.5
  73.7 0.7 copy.26.gw
  74.5 24.2 %shard_map.92 = bf16[128,2048]{1,0:T(8,128)(2,1)} custom-call(s32[4,16]{1,0:T(4,128)} %bitcast.27, bf16[128,3072]{1,0:T(8,128)(2,1)} %q.1, bf16[128,64,128]{2,1,0:T(8,128)(2,1)} %bitcast.15, bf16[128,64,128]{2,1,0:T(8,128)(2,1)} %bitcast.16, bf16[128,32,128]{2,1,0:T(8,128)(2,1)} %bitcast.18, bf16[8,128,128]{2,1,0:T(8,128)(2,1)} %get-tuple-element.16.nkh, ...), custom_call_target="tpu_custom_call" | custom-call | tf_op jit(solution)/shard_map/pallas_call | solution.py:795
  (6 shorter events, 0.1 us)
Async XLA Ops:
  0.0 2.1 %copy-start.4 = (bf16[128,192]{0,1:T(8,128)(2,1)S(1)}, bf16[128,192]{0,1:T(8,128)(2,1)}, u32[]{:S(2)}) copy-start(bf16[128,192]{0,1:T(8,128)(2,1)} %param.12) | copy-start | bytes 147460
  0.0 4.2 %copy-start.2 = (bf16[1536,192]{0,1:T(8,128)(2,1)S(1)}, bf16[1536,192]{0,1:T(8,128)(2,1)}, u32[]{:S(2)}) copy-start(bf16[1536,192]{0,1:T(8,128)(2,1)} %param.14) | copy-start | bytes 1769476
  1.3 5.0 %copy-start = (bf16[1024,192]{1,0:T(8,128)(2,1)}, bf16[1024,192]{1,0:T(8,128)(2,1)S(1)}, u32[]{:S(2)}) copy-start(bf16[1024,192]{1,0:T(8,128)(2,1)S(1)} %copy.22.ck) | copy-start | bytes 1179652
  1.3 4.2 %copy-start.1 = (bf16[1024,128]{1,0:T(8,128)(2,1)S(1)}, bf16[1024,128]{1,0:T(8,128)(2,1)}, u32[]{:S(2)}) copy-start(bf16[1024,128]{1,0:T(8,128)(2,1)} %cv.1) | copy-start | bytes 786436
  2.2 4.0 %copy-start.3 = (bf16[128,192]{1,0:T(8,128)(2,1)}, bf16[128,192]{1,0:T(8,128)(2,1)S(1)}, u32[]{:S(2)}) copy-start(bf16[128,192]{1,0:T(8,128)(2,1)S(1)} %copy.23.ik) | copy-start | bytes 147460
  4.2 69.4 %copy-start.5 = (bf16[16,192,3]{1,0,2:T(8,128)(2,1)S(1)}, bf16[16,192,3]{1,0,2:T(8,128)(2,1)}, u32[]{:S(2)}) copy-start(bf16[16,192,3]{1,0,2:T(8,128)(2,1)} %param.17) | copy-start | bytes 55300

commit v2 on v0

--- a/solution.py
+++ b/solution.py
@@ -1,6 +1,10 @@
+import functools
+
 import jax
 import jax.numpy as jnp
 from jax import lax
+from jax.experimental import pallas as pl
+from jax.experimental.pallas import tpu as pltpu
 from jax.sharding import PartitionSpec as P
 
 CMP_STRIDE = 16
@@ -41,7 +45,7 @@
     return mixed / total
 
 
-def shards(
+def shards_by_request(
     queries,
     cache_keys,
     cache_values,
@@ -219,6 +223,638 @@
     return mixed.astype(jnp.bfloat16).reshape(query_count, heads * value_width)
 
 
+CORES = 2
+LOG2E = 1.4426950408889634
+MESH = pl.DeviceIdType.MESH
+
+
+def fused_kernel(
+    n_seq,
+    n_kv,
+    tiles,
+    sel,
+    q,
+    ckt,
+    cv,
+    ikt,
+    iv,
+    wkt,
+    wv,
+    gw,
+    out,
+    q_vm,
+    ckt_vm,
+    ikt_vm,
+    gw_vm,
+    kh,
+    v,
+    kl,
+    nkh,
+    nv,
+    nkl,
+    k_ext,
+    v_ext,
+    perm,
+    lhs_k,
+    lhs_v,
+    wk_all,
+    wv_all,
+    compk_vm,
+    compv_vm,
+    compk,
+    compv,
+    rows_vm,
+    gates_vm,
+    acc,
+    win_k,
+    win_v,
+    sel_k,
+    sel_v,
+    local_sem,
+    own_sem,
+    kv_send,
+    kv_recv,
+    new_send,
+    new_recv,
+    w_send,
+    w_recv,
+    comp_send,
+    comp_recv,
+):
+    me = lax.axis_index("seq")
+    group = lax.axis_index("kv")
+    z = me // CORES
+    core = lax.rem(me, CORES)
+    chips = n_seq // CORES
+    mate = z * CORES + 1 - core
+    left = lax.rem(me - CORES + n_seq, n_seq)
+    right = lax.rem(me + CORES, n_seq)
+    route = (left, right, mate)
+    width, cache = ckt.shape
+    fresh = ikt.shape[1]
+    vw = v.shape[2]
+    low = width - vw
+    per = cache // SEL_BLOCK
+    new_per = fresh // SEL_BLOCK
+    half_block = SEL_BLOCK // 2
+    heads = q.shape[1] // width
+    tile = fresh // tiles
+    count = heads * tile
+    lookback = WINDOW // fresh
+    hops = -(-lookback // CORES)
+    chunks = cache // CMP_STRIDE
+    pad = chunks + CMP_STRIDE
+    factor = width**-0.5 * LOG2E
+
+    barrier = pltpu.get_barrier_semaphore()
+    for d in range(1, n_seq):
+        pl.semaphore_signal(
+            barrier, inc=1, device_id={"seq": lax.rem(me + d, n_seq)}, device_id_type=MESH
+        )
+    for d in range(1, n_kv):
+        pl.semaphore_signal(
+            barrier, inc=1, device_id={"kv": lax.rem(group + d, n_kv)}, device_id_type=MESH
+        )
+
+    half_k = wkt.shape[1] // CORES
+    half_v = wv.shape[0] // CORES
+    loads = [
+        (cv, v.at[pl.ds(me * per, per)]),
+        (iv, nv.at[pl.ds(me * new_per, new_per)]),
+        (ckt, ckt_vm),
+        (ikt, ikt_vm),
+        (q, q_vm),
+        (gw, gw_vm),
+    ]
+    for half in range(CORES):
+        loads.append((wkt.at[:, pl.ds(half * half_k, half_k)], wk_all.at[group, half]))
+        loads.append((wv.at[pl.ds(half * half_v, half_v)], wv_all.at[group, half]))
+    load_copies = [pltpu.make_async_copy(a, b, local_sem.at[n]) for n, (a, b) in enumerate(loads)]
+    for copy in load_copies:
+        copy.start()
+
+    old = (v, kh, kl)
+    new = (nv, nkh, nkl)
+
+    def piece(half):
+        return per // 2 * half, per // 2
+
+    def old_msg(slot, way, part, half):
+        at, size = piece(half)
+        ref = old[part].at[pl.ds(slot * per + at, size)]
+        return pltpu.make_async_remote_copy(
+            src_ref=ref,
+            dst_ref=ref,
+            send_sem=kv_send.at[way, slot, part, half],
+            recv_sem=kv_recv.at[slot, part, half],
+            device_id={"seq": route[way]},
+            device_id_type=MESH,
+        )
+
+    def new_msg(slot, way, part, half):
+        ref = new[part].at[pl.ds(slot * new_per, new_per)]
+        return pltpu.make_async_remote_copy(
+            src_ref=ref,
+            dst_ref=ref,
+            send_sem=new_send.at[way, slot, part],
+            recv_sem=new_recv.at[slot, part],
+            device_id={"seq": route[way]},
+            device_id_type=MESH,
+        )
+
+    def start(make, slot, way, half, parts=range(3)):
+        for part in parts:
+            make(slot, way, part, half).start()
+
+    def recv(make, slot, half):
+        for part in range(3):
+            make(slot, 2, part, half).wait_recv()
+
+    def sent(make, slot, way, half):
+        for part in range(3):
+            make(slot, way, part, half).wait_send()
+
+    def start_own(parts):
+        for half in (1, 0):
+
+            @pl.when(z < chips - 1)
+            def _():
+                start(old_msg, me, 1, half, parts)
+
+            @pl.when(z > 0)
+            def _():
+                start(old_msg, me, 0, half, parts)
+
+            start(old_msg, me, 2, half, parts)
+
+    w_all = (wk_all, wv_all)
+    w_own = (
+        wkt.at[:, pl.ds(pl.multiple_of(core * half_k, half_k), half_k)],
+        wv.at[pl.ds(pl.multiple_of(core * half_v, half_v), half_v)],
+    )
+
+    def w_msg(d, part):
+        return pltpu.make_async_remote_copy(
+            src_ref=w_own[part],
+            dst_ref=w_all[part].at[group, core],
+            send_sem=w_send.at[d - 1, part],
+            recv_sem=w_recv.at[group, core, part],
+            device_id={"kv": lax.rem(group + d, n_kv)},
+            device_id_type=MESH,
+        )
+
+    def w_arrived(who, half, part):
+        return pltpu.make_async_remote_copy(
+            src_ref=w_all[part].at[who, half],
+            dst_ref=w_all[part].at[who, half],
+            send_sem=w_send.at[n_kv - 1 + lax.rem(who - group + n_kv, n_kv) - 1, part],
+            recv_sem=w_recv.at[who, half, part],
+            device_id={"seq": mate},
+            device_id_type=MESH,
+        )
+
+    load_copies[0].wait()
+    load_copies[1].wait()
+    pl.semaphore_wait(barrier, n_seq - 1 + n_kv - 1)
+    start_own((0,))
+    for d in range(1, n_kv):
+        for part in range(2):
+            w_msg(d, part).start()
+
+    def pack(keys, blocks, hi, lo, at):
+        hi[pl.ds(at, blocks)] = keys[:, 0:vw].reshape(blocks, SEL_BLOCK, vw)
+        part = keys[:, vw:width].reshape(blocks, 2, half_block, low)
+        lo[pl.ds(at, blocks)] = jnp.concatenate([part[:, 0], part[:, 1]], axis=-1)
+
+    load_copies[2].wait()
+    keys = ckt_vm[...].T
+    pack(keys, per, kh, kl, me * per)
+    k_ext[CMP_STRIDE:, :] = keys
+    load_copies[3].wait()
+    pack(ikt_vm[...].T, new_per, nkh, nkl, me * new_per)
+    v_ext[CMP_STRIDE:, :] = v[pl.ds(me * per, per)].reshape(cache, vw)
+    for copy in load_copies[4:]:
+        copy.wait()
+
+    @pl.when(z < chips - 1)
+    def _():
+        start(new_msg, me, 1, 0)
+
+    start_own((1, 2))
+    start(new_msg, me, 2, 0)
+
+    @pl.loop(0, tiles)
+    def _(t):
+        part = q_vm[pl.ds(pl.multiple_of(t * tile, tile), tile), :]
+        for h in range(heads):
+            at = pl.multiple_of(t * count + h * tile, tile)
+            rows_vm[pl.ds(at, tile), :] = part[:, h * width : (h + 1) * width]
+
+    logits = lax.dot_general(
+        rows_vm[...], gw_vm[...], (((1,), (1,)), ((), ())), preferred_element_type=jnp.float32
+    )
+    gates_vm[...] = jax.nn.sigmoid(logits)
+    lag = lax.broadcasted_iota(jnp.int32, (pad, cache + CMP_STRIDE), 1)
+    lag = lag - CMP_STRIDE * lax.broadcasted_iota(jnp.int32, lag.shape, 0)
+
+    @pl.loop(0, CMP_STRIDE)
+    def _(p):
+        at = pl.multiple_of(p * pad, CMP_STRIDE)
+        perm[pl.ds(at, pad), :] = jnp.where(lag == p, 1.0, 0.0).astype(jnp.bfloat16)
+
+    for d in range(1, min(hops, chips - 1) + 1):
+
+        @pl.when(z >= d)
+        def _():
+            slot = me - CORES * d
+            recv(new_msg, slot, 0)
+            if d < hops:
+
+                @pl.when(z < chips - 1)
+                def _():
+                    start(new_msg, slot, 1, 0)
+
+            start(new_msg, slot, 2, 0)
+
+    def relay(d, half):
+        @pl.when(z >= d)
+        def _():
+            slot = me - CORES * d
+            recv(old_msg, slot, half)
+
+            @pl.when(z < chips - 1)
+            def _():
+                start(old_msg, slot, 1, half)
+
+            start(old_msg, slot, 2, half)
+
+        @pl.when(z + d < chips)
+        def _():
+            slot = me + CORES * d
+            recv(old_msg, slot, half)
+
+            @pl.when(z > 0)
+            def _():
+                start(old_msg, slot, 0, half)
+
+            start(old_msg, slot, 2, half)
+
+    comps = ((compk_vm, compk), (compv_vm, compv))
+
+    def comp_msg(d, part, who):
+        return pltpu.make_async_remote_copy(
+            src_ref=comps[part][0],
+            dst_ref=comps[part][1].at[who],
+            send_sem=comp_send.at[d - 1, part],
+            recv_sem=comp_recv.at[who, part],
+            device_id={"seq": lax.rem(me + d, n_seq)},
+            device_id_type=MESH,
+        )
+
+    def comp_keep(part):
+        return pltpu.make_async_copy(comps[part][0], comps[part][1].at[me], own_sem.at[part])
+
+    def spread_tokens():
+        tail = SEL_BLOCK - CMP_STRIDE
+
+        @pl.when(me > 0)
+        def _():
+            recv(old_msg, me - 1, 1)
+            block = me * per - 1
+            k_ext[0:CMP_STRIDE, 0:vw] = kh[block, tail:SEL_BLOCK]
+            k_ext[0:CMP_STRIDE, vw:width] = kl[block, tail - half_block : half_block, low:]
+            v_ext[0:CMP_STRIDE, :] = v[block, tail:SEL_BLOCK]
+
+        @pl.when(me == 0)
+        def _():
+            k_ext[0:CMP_STRIDE, :] = jnp.zeros((CMP_STRIDE, width), jnp.bfloat16)
+            v_ext[0:CMP_STRIDE, :] = jnp.zeros((CMP_STRIDE, vw), jnp.bfloat16)
+
+        for lhs, ext in ((lhs_k, k_ext), (lhs_v, v_ext)):
+            spread = jnp.dot(perm[...], ext[...], preferred_element_type=jnp.float32)
+            spread = spread.astype(jnp.bfloat16)
+            each = ext.shape[1]
+            for p in range(CMP_STRIDE):
+                lhs[:, p * each : (p + 1) * each] = spread[p * pad : (p + 1) * pad]
+
+    def pass_weights():
+        for d in range(1, n_kv):
+            who = lax.rem(group + n_kv - d, n_kv)
+            for part in range(2):
+                w_arrived(who, core, part).wait_recv()
+                w_arrived(who, core, part).start()
+
+    def compress():
+        for d in range(1, n_kv):
+            who = lax.rem(group + n_kv - d, n_kv)
+            for part in range(2):
+                w_arrived(who, 1 - core, part).wait_recv()
+        for lhs, w, held, dims in (
+            (lhs_k, wk_all, compk_vm, (((1,), (1,)), ((), ()))),
+            (lhs_v, wv_all, compv_vm, (((1,), (0,)), ((), ()))),
+        ):
+            pieces = n_kv * CORES // 2
+            depth = lhs.shape[1] // pieces
+            sums = []
+            for side in range(2):
+                total = None
+                for n in range(pieces):
+                    at = side * pieces + n
+                    term = lax.dot_general(
+                        lhs[:, n * depth : (n + 1) * depth],
+                        w[at // CORES, at % CORES],
+                        dims,
+                        preferred_element_type=jnp.float32,
+                    )
+                    total = term if total is None else total + term
+                sums.append(total)
+            held[...] = (sums[0][0:chunks] + sums[1][1 : chunks + 1]).astype(jnp.bfloat16)
+        for part in range(2):
+            comp_keep(part).start()
+        for d in range(1, n_seq):
+            for part in range(2):
+                comp_msg(d, part, me).start()
+
+    def attend(rows, keys, values, allowed):
+        s = lax.dot_general(
+            rows, keys, (((1,), (1,)), ((), ())), preferred_element_type=jnp.float32
+        )
+        if allowed is not None:
+            s = jnp.where(allowed, s, MASKED)
+        top = jnp.max(s, axis=-1, keepdims=True)
+        w = jnp.exp2((s - top) * factor)
+        total = jnp.sum(w, axis=-1, keepdims=True)
+        o = jnp.dot(w.astype(jnp.bfloat16), values, preferred_element_type=jnp.float32)
+        return o / total
+
+    def gated(branch, t, o, emit):
+        g = gates_vm[pl.ds(pl.multiple_of(t * count, count), count), :]
+        for h in range(heads):
+            a = slice(h * tile, (h + 1) * tile)
+            at = branch * heads + h
+            emit(h, pl.ds(pl.multiple_of(t * count + h * tile, tile), tile), g[a, at : at + 1] * o[a])
+
+    def rows_of(t):
+        return rows_vm[pl.ds(pl.multiple_of(t * count, count), count), :]
+
+    def compressed():
+        for part in range(2):
+            comp_keep(part).wait()
+        for d in range(1, n_seq):
+            who = lax.rem(me + d, n_seq)
+            for part in range(2):
+                comp_msg(d, part, who).wait_recv()
+        total = n_seq * chunks
+        ok = lax.broadcasted_iota(jnp.int32, (count, total), 1) > 0
+
+        @pl.loop(0, tiles)
+        def _(t):
+            o = attend(
+                rows_of(t),
+                compk[...].reshape(total, width),
+                compv[...].reshape(total, vw),
+                ok,
+            )
+
+            def emit(h, at, x):
+                acc[at, :] = x
+
+            gated(0, t, o, emit)
+
+    def put(dk, dv, at, khv, vv, klv):
+        dk[pl.ds(at, SEL_BLOCK), 0:vw] = khv
+        dk[pl.ds(at, half_block), vw:width] = klv[:, 0:low]
+        dk[pl.ds(at + half_block, half_block), vw:width] = klv[:, low : 2 * low]
+        dv[pl.ds(at, SEL_BLOCK), :] = vv
+
+    def window():
+        @pl.when(core == 0)
+        def _():
+            recv(old_msg, n_seq - 1, 1)
+
+        for d in range(0, min(hops, chips - 1) + 1):
+
+            @pl.when(z >= d)
+            def _():
+                recv(new_msg, (z - d) * CORES + 1 - core, 0)
+
+        for i in range(lookback + 1):
+            chunk = me + i
+            for b in range(new_per):
+                at = (i * new_per + b) * SEL_BLOCK
+
+                @pl.when(chunk < lookback)
+                def _():
+                    block = n_seq * per - lookback * new_per + chunk * new_per + b
+                    put(win_k, win_v, at, kh[block], v[block], kl[block])
+
+                @pl.when(chunk >= lookback)
+                def _():
+                    block = (chunk - lookback) * new_per + b
+                    put(win_k, win_v, at, nkh[block], nv[block], nkl[block])
+
+        span = WINDOW + tile
+        diff = lax.broadcasted_iota(jnp.int32, (count, span), 1) - lax.rem(
+            lax.broadcasted_iota(jnp.int32, (count, span), 0), tile
+        )
+        ok = (diff > 0) & (diff <= WINDOW)
+
+        @pl.loop(0, tiles)
+        def _(t):
+            off = pl.multiple_of(t * tile, tile)
+            o = attend(rows_of(t), win_k[pl.ds(off, span), :], win_v[pl.ds(off, span), :], ok)
+
+            def emit(h, at, x):
+                acc[at, :] += x
+
+            gated(2, t, o, emit)
+
+    def selected():
+        picks = sel.shape[1]
+
+        @pl.loop(0, tiles)
+        def _(t):
+            for n in range(picks):
+                block = sel[t, n]
+                put(sel_k, sel_v, n * SEL_BLOCK, kh[block], v[block], kl[block])
+            o = attend(rows_of(t), sel_k[...], sel_v[...], None)
+
+            def emit(h, at, x):
+                to = pl.ds(pl.multiple_of(t * tile, tile), tile)
+                out[to, h * vw : (h + 1) * vw] = (acc[at, :] + x).astype(out.dtype)
+
+            gated(1, t, o, emit)
+
+    relay(1, 1)
+    relay(1, 0)
+    spread_tokens()
+    pass_weights()
+    for d in range(2, chips - 1):
+        relay(d, 1)
+    compress()
+    for d in range(2, chips - 1):
+        relay(d, 0)
+    compressed()
+    relay(chips - 1, 1)
+    window()
+    relay(chips - 1, 0)
+
+    for zz in range(chips):
+        slot = zz * CORES + 1 - core
+        recv(old_msg, slot, 0)
+        early = slot == me - 1
+        if zz == chips - 1:
+            early = early | (core == 0)
+
+        @pl.when(jnp.logical_not(early))
+        def _():
+            recv(old_msg, slot, 1)
+
+    selected()
+
+    for d in range(1, n_kv):
+        for part in range(2):
+            w_msg(d, part).wait_send()
+            w_arrived(lax.rem(group + n_kv - d, n_kv), core, part).wait_send()
+    for d in range(1, n_seq):
+        for part in range(2):
+            comp_msg(d, part, me).wait_send()
+
+    def all_sent(slot, ways):
+        for way in ways:
+            for half in range(2):
+                sent(old_msg, slot, way, half)
+
+    @pl.when(z < chips - 1)
+    def _():
+        sent(new_msg, me, 1, 0)
+        all_sent(me, (1,))
+
+    @pl.when(z > 0)
+    def _():
+        all_sent(me, (0,))
+
+    sent(new_msg, me, 2, 0)
+    all_sent(me, (2,))
+    for d in range(1, chips):
+
+        @pl.when(z >= d)
+        def _():
+            slot = me - CORES * d
+            if d <= hops:
+                sent(new_msg, slot, 2, 0)
+
+                if d < hops:
+
+                    @pl.when(z < chips - 1)
+                    def _():
+                        sent(new_msg, slot, 1, 0)
+
+            all_sent(slot, (2,))
+
+            @pl.when(z < chips - 1)
+            def _():
+                all_sent(slot, (1,))
+
+        @pl.when(z + d < chips)
+        def _():
+            slot = me + CORES * d
+            all_sent(slot, (2,))
+
+            @pl.when(z > 0)
+            def _():
+                all_sent(slot, (0,))
+
+
+def shards_gathered(q, ck, cv, ik, iv, wk, wv, sel, gw):
+    n_seq, n_kv = lax.axis_size("seq"), lax.axis_size("kv")
+    heads, width, branches = gw.shape
+    vw = cv.shape[1]
+    cache, fresh = ck.shape[0], ik.shape[0]
+    tiles, picks = sel.shape[0], sel.shape[-1]
+    chunks = cache // CMP_STRIDE
+    pad = chunks + CMP_STRIDE
+    per, new_per = cache // SEL_BLOCK, fresh // SEL_BLOCK
+    tile_rows = heads * fresh
+    bf = jnp.bfloat16
+    any_spec = pl.BlockSpec(memory_space=pl.ANY)
+    half_k, half_v = wk.shape[0] // CORES, wv.shape[0] // CORES
+
+    def held(*shape):
+        return pltpu.VMEM(shape, bf)
+
+    dma = pltpu.SemaphoreType.DMA
+    return pl.pallas_call(
+        functools.partial(fused_kernel, n_seq, n_kv, tiles),
+        out_shape=jax.ShapeDtypeStruct((fresh, heads * vw), bf),
+        in_specs=[pl.BlockSpec(memory_space=pltpu.SMEM)] + [any_spec] * 8,
+        out_specs=pl.BlockSpec(memory_space=pltpu.VMEM),
+        scratch_shapes=[
+            held(*q.shape),
+            held(width, cache),
+            held(width, fresh),
+            held(heads * branches, width),
+            held(n_seq * per, SEL_BLOCK, vw),
+            held(n_seq * per, SEL_BLOCK, vw),
+            held(n_seq * per, SEL_BLOCK // 2, vw),
+            held(n_seq * new_per, SEL_BLOCK, vw),
+            held(n_seq * new_per, SEL_BLOCK, vw),
+            held(n_seq * new_per, SEL_BLOCK // 2, vw),
+            held(cache + CMP_STRIDE, width),
+            held(cache + CMP_STRIDE, vw),
+            held(CMP_STRIDE * pad, cache + CMP_STRIDE),
+            held(pad, CMP_STRIDE * width),
+            held(pad, CMP_STRIDE * vw),
+            held(n_kv, CORES, width, half_k),
+            held(n_kv, CORES, half_v, vw),
+            held(chunks, width),
+            held(chunks, vw),
+            held(n_seq, chunks, width),
+            held(n_seq, chunks, vw),
+            held(tile_rows, width),
+            pltpu.VMEM((tile_rows, heads * branches), jnp.float32),
+            pltpu.VMEM((tile_rows, vw), jnp.float32),
+            held(fresh + WINDOW, width),
+            held(fresh + WINDOW, vw),
+            held(picks * SEL_BLOCK, width),
+            held(picks * SEL_BLOCK, vw),
+            dma((6 + 2 * CORES,)),
+            dma((2,)),
+            dma((3, n_seq, 3, 2)),
+            dma((n_seq, 3, 2)),
+            dma((3, n_seq, 3)),
+            dma((n_seq, 3)),
+            dma((2 * (n_kv - 1), 2)),
+            dma((n_kv, CORES, 2)),
+            dma((n_seq - 1, 2)),
+            dma((n_seq, 2)),
+        ],
+        compiler_params=pltpu.CompilerParams(
+            collective_id=0, has_side_effects=True, vmem_limit_bytes=60 << 20
+        ),
+    )(
+        sel.reshape(tiles, picks),
+        q,
+        ck.T,
+        cv.reshape(per, SEL_BLOCK, vw),
+        ik.T,
+        iv.reshape(new_per, SEL_BLOCK, vw),
+        wk.T,
+        wv,
+        jnp.transpose(gw, (2, 0, 1)).reshape(heads * branches, width),
+    )
+
+
+GATHER_BYTES = 1 << 24
+
+
+def shards(queries, cache_keys, cache_values, *rest):
+    ranks = lax.axis_size("seq")
+    size = ranks * 2 * (cache_keys.size + cache_values.size)
+    form = shards_gathered if size <= GATHER_BYTES else shards_by_request
+    return form(queries, cache_keys, cache_values, *rest)
+
+
 def solution(mesh):
     placed = (
         P("seq", "kv"),

time: 312 us -> 73.4 us (0.24)
  blocking collectives: 102 us -> 0 us
  Pallas kernels: 0 us -> 70.1 us
  local copies, waits for them, and re-layouts: 62.7 us -> 1.88 us
  starting transfers between devices: 54.2 us -> 0 us
  waiting for transfers between devices: 44.2 us -> 0 us
  matrix products: 18.3 us -> 0 us
  other arithmetic: 14.3 us -> 0 us
  between operations: 14 us -> 0.01 us
    all_gather x2 -> x0, blocking collectives: 102 us -> none  [the longest x1 88 us: shards(): values = lax.all_gather(comp_values, 'seq', axis=0, tiled=True)]
    pallas_call x0 -> x1, Pallas kernels: none -> 70.1 us  [shards_gathered(): pl.pallas_call(functools.partial(fused_kernel, n_seq, n_kv, tiles), out_s...]
    ppermute x5 -> x0, waiting for transfers between devices: 42.7 us -> none  [the longest x4 42.7 us: from_behind(): return lax.ppermute(x, axis, pairs)]
    all_to_all x3 -> x0, starting transfers between devices: 38.7 us -> none  [the longest x1 29.5 us: shards(): lax.all_to_all(key_blocks[safe], 'seq', split_axis=0, concat_axis=0, tile...]
    dot_general x11 -> x0, matrix products: 18.3 us -> none  [the longest x2 4.96 us: finish_rows(): jnp.matmul(weights.astype(jnp.bfloat16), values, preferred_element_type=j...]
    ppermute x5 -> x0, starting transfers between devices: 15.5 us -> none  [the longest x4 12.8 us: from_behind(): return lax.ppermute(x, axis, pairs)]
    reshape x17 -> x0, local copies, waits for them, and re-layouts: 11.4 us -> none  [the longest x1 2.15 us: shards(): rows = queries.reshape(query_count * heads, key_width)]
    gather x4 -> x0, local copies, waits for them, and re-layouts: 11.3 us -> none  [the longest x1 3.39 us: shards(): got_values.reshape(ranks * capacity, SEL_BLOCK, value_width)[where_at]]
  transfers between devices with their start and end apart: 10 -> 0, of which waited for: 4 -> 0; matrix products, arithmetic and copies ran while one was open for 26% -> 0% of each run, Pallas kernels for 0% -> 0%
where the time goes in v2:
time: 73.4 us; the launch traced here: 72 us
  Pallas kernels  70.1 us (96%)
  local copies, waits for them, and re-layouts  1.88 us (3%)
    pallas_call x1, Pallas kernels, shards_gathered(): pl.pallas_call(functools.partial(fused_kernel, n_seq, n_kv, tiles), out_s...  70.1 us
    unnamed x1, local copies, waits for them, and re-layouts  1.88 us

profile of v2, /device:TPU:1, one launch (start us, length us, event | category | flops | bytes accessed | tf_op | source)
XLA Modules:
  0.0 72.0 jit_solution(1437709347411796229)
XLA Ops:
  0.0 70.1 %shard_map.91 = bf16[128,2048]{1,0:T(8,128)(2,1)} custom-call(s32[4,16]{1,0:T(4,128)} %bitcast.15, bf16[128,3072]{1,0:T(8,128)(2,1)} %q.1, bf16[192,1024]{1,0:T(8,128)(2,1)} %bitcast.10, bf16[16,64,128]{2,1,0:T(8,128)(2,1)} %bitcast.11, bf16[192,128]{1,0:T(8,128)(2,1)} %bitcast.12, bf16[2,64,128]{2,1,0:T(8,128)(2,1)} %bitcast.13, bf16[192,1536]{1,0:T(8,128)(2,1)} %bitcast.9, ...), custom_call_target="tpu_custom_call" | custom-call | tf_op jit(solution)/shard_map/pallas_call | solution.py:787
  70.1 1.9 %copy.11 = bf16[128,2048]{1,0:T(8,128)(2,1)} copy(bf16[128,2048]{1,0:T(8,128)(2,1)} %shard_map.91) | data formatting | bytes 1048576

commit v3 on v2

--- a/solution.py
+++ b/solution.py
@@ -224,6 +224,7 @@
 
 
 CORES = 2
+PIECES = 4
 LOG2E = 1.4426950408889634
 MESH = pl.DeviceIdType.MESH
 
@@ -259,8 +260,8 @@
     lhs_v,
     wk_all,
     wv_all,
-    compk_vm,
-    compv_vm,
+    comp_vm,
+    comp_all,
     compk,
     compv,
     rows_vm,
@@ -336,17 +337,17 @@
     old = (v, kh, kl)
     new = (nv, nkh, nkl)
 
-    def piece(half):
-        return per // 2 * half, per // 2
-
-    def old_msg(slot, way, part, half):
-        at, size = piece(half)
-        ref = old[part].at[pl.ds(slot * per + at, size)]
+    def pieces_of(half):
+        return range(PIECES // 2 * half, PIECES // 2 * (half + 1))[::-1]
+
+    def old_msg(slot, way, part, piece):
+        size = per // PIECES
+        ref = old[part].at[pl.ds(slot * per + piece * size, size)]
         return pltpu.make_async_remote_copy(
             src_ref=ref,
             dst_ref=ref,
-            send_sem=kv_send.at[way, slot, part, half],
-            recv_sem=kv_recv.at[slot, part, half],
+            send_sem=kv_send.at[way, slot, part, piece],
+            recv_sem=kv_recv.at[slot, part, piece],
             device_id={"seq": route[way]},
             device_id_type=MESH,
         )
@@ -375,7 +376,7 @@
             make(slot, way, part, half).wait_send()
 
     def start_own(parts):
-        for half in (1, 0):
+        for half in range(PIECES)[::-1]:
 
             @pl.when(z < chips - 1)
             def _():
@@ -476,7 +477,15 @@
 
             start(new_msg, slot, 2, 0)
 
-    def relay(d, half):
+    def relay(d, side):
+        for piece in pieces_of(side):
+            relay_piece(d, piece)
+
+    def recv_side(slot, side):
+        for piece in pieces_of(side):
+            recv(old_msg, slot, piece)
+
+    def relay_piece(d, half):
         @pl.when(z >= d)
         def _():
             slot = me - CORES * d
@@ -499,27 +508,46 @@
 
             start(old_msg, slot, 2, half)
 
-    comps = ((compk_vm, compk), (compv_vm, compv))
-
-    def comp_msg(d, part, who):
+    def comp_send_own(d):
+        to = lax.rem(me + CORES * d, n_seq) if d else mate
         return pltpu.make_async_remote_copy(
-            src_ref=comps[part][0],
-            dst_ref=comps[part][1].at[who],
-            send_sem=comp_send.at[d - 1, part],
-            recv_sem=comp_recv.at[who, part],
-            device_id={"seq": lax.rem(me + d, n_seq)},
+            src_ref=comp_vm,
+            dst_ref=comp_all.at[me],
+            send_sem=comp_send.at[d],
+            recv_sem=comp_recv.at[me],
+            device_id={"seq": to},
             device_id_type=MESH,
         )
 
-    def comp_keep(part):
-        return pltpu.make_async_copy(comps[part][0], comps[part][1].at[me], own_sem.at[part])
+    def comp_pass(d):
+        who = lax.rem(me + CORES * d, n_seq)
+        return pltpu.make_async_remote_copy(
+            src_ref=comp_all.at[who],
+            dst_ref=comp_all.at[who],
+            send_sem=comp_send.at[chips + d - 1],
+            recv_sem=comp_recv.at[who],
+            device_id={"seq": mate},
+            device_id_type=MESH,
+        )
+
+    def comp_take(who):
+        return pltpu.make_async_remote_copy(
+            src_ref=comp_all.at[who],
+            dst_ref=comp_all.at[who],
+            send_sem=comp_send.at[0],
+            recv_sem=comp_recv.at[who],
+            device_id={"seq": mate},
+            device_id_type=MESH,
+        )
+
+    comp_keep = pltpu.make_async_copy(comp_vm, comp_all.at[me], own_sem)
 
     def spread_tokens():
         tail = SEL_BLOCK - CMP_STRIDE
 
         @pl.when(me > 0)
         def _():
-            recv(old_msg, me - 1, 1)
+            recv_side(me - 1, 1)
             block = me * per - 1
             k_ext[0:CMP_STRIDE, 0:vw] = kh[block, tail:SEL_BLOCK]
             k_ext[0:CMP_STRIDE, vw:width] = kl[block, tail - half_block : half_block, low:]
@@ -549,9 +577,10 @@
             who = lax.rem(group + n_kv - d, n_kv)
             for part in range(2):
                 w_arrived(who, 1 - core, part).wait_recv()
-        for lhs, w, held, dims in (
-            (lhs_k, wk_all, compk_vm, (((1,), (1,)), ((), ()))),
-            (lhs_v, wv_all, compv_vm, (((1,), (0,)), ((), ()))),
+        results = []
+        for lhs, w, dims in (
+            (lhs_k, wk_all, (((1,), (1,)), ((), ()))),
+            (lhs_v, wv_all, (((1,), (0,)), ((), ()))),
         ):
             pieces = n_kv * CORES // 2
             depth = lhs.shape[1] // pieces
@@ -568,12 +597,17 @@
                     )
                     total = term if total is None else total + term
                 sums.append(total)
-            held[...] = (sums[0][0:chunks] + sums[1][1 : chunks + 1]).astype(jnp.bfloat16)
-        for part in range(2):
-            comp_keep(part).start()
-        for d in range(1, n_seq):
-            for part in range(2):
-                comp_msg(d, part, me).start()
+            results.append((sums[0][0:chunks] + sums[1][1 : chunks + 1]).astype(jnp.bfloat16))
+        made, made_v = results
+        comp_vm[0:chunks, :] = made[:, 0:vw]
+        comp_vm[chunks : 2 * chunks, :] = made_v
+        comp_vm[2 * chunks :, :] = jnp.concatenate(
+            [made[0 : chunks // 2, vw:width], made[chunks // 2 :, vw:width]], axis=-1
+        )
+        for d in range(1, chips):
+            comp_send_own(d).start()
+        comp_send_own(0).start()
+        comp_keep.start()
 
     def attend(rows, keys, values, allowed):
         s = lax.dot_general(
@@ -598,21 +632,27 @@
         return rows_vm[pl.ds(pl.multiple_of(t * count, count), count), :]
 
     def compressed():
-        for part in range(2):
-            comp_keep(part).wait()
-        for d in range(1, n_seq):
-            who = lax.rem(me + d, n_seq)
-            for part in range(2):
-                comp_msg(d, part, who).wait_recv()
+        comp_keep.wait()
+        for d in range(1, chips):
+            comp_pass(d).wait_recv()
+            comp_pass(d).start()
+        for zz in range(chips):
+            comp_take(zz * CORES + 1 - core).wait_recv()
         total = n_seq * chunks
+        for slot in range(n_seq):
+            at, mid = slot * chunks, slot * chunks + chunks // 2
+            compk[at : at + chunks, 0:vw] = comp_all[slot, 0:chunks]
+            compk[at:mid, vw:width] = comp_all[slot, 2 * chunks :, 0:low]
+            compk[mid : at + chunks, vw:width] = comp_all[slot, 2 * chunks :, low : 2 * low]
+            compv[at : at + chunks, :] = comp_all[slot, chunks : 2 * chunks]
         ok = lax.broadcasted_iota(jnp.int32, (count, total), 1) > 0
 
         @pl.loop(0, tiles)
         def _(t):
             o = attend(
                 rows_of(t),
-                compk[...].reshape(total, width),
-                compv[...].reshape(total, vw),
+                compk[...],
+                compv[...],
                 ok,
             )
 
@@ -630,7 +670,7 @@
     def window():
         @pl.when(core == 0)
         def _():
-            recv(old_msg, n_seq - 1, 1)
+            recv_side(n_seq - 1, 1)
 
         for d in range(0, min(hops, chips - 1) + 1):
 
@@ -689,10 +729,9 @@
     relay(1, 0)
     spread_tokens()
     pass_weights()
+    compress()
     for d in range(2, chips - 1):
         relay(d, 1)
-    compress()
-    for d in range(2, chips - 1):
         relay(d, 0)
     compressed()
     relay(chips - 1, 1)
@@ -701,14 +740,14 @@
 
     for zz in range(chips):
         slot = zz * CORES + 1 - core
-        recv(old_msg, slot, 0)
+        recv_side(slot, 0)
         early = slot == me - 1
         if zz == chips - 1:
             early = early | (core == 0)
 
         @pl.when(jnp.logical_not(early))
         def _():
-            recv(old_msg, slot, 1)
+            recv_side(slot, 1)
 
     selected()
 
@@ -716,13 +755,14 @@
         for part in range(2):
             w_msg(d, part).wait_send()
             w_arrived(lax.rem(group + n_kv - d, n_kv), core, part).wait_send()
-    for d in range(1, n_seq):
-        for part in range(2):
-            comp_msg(d, part, me).wait_send()
+    for d in range(0, chips):
+        comp_send_own(d).wait_send()
+    for d in range(1, chips):
+        comp_pass(d).wait_send()
 
     def all_sent(slot, ways):
         for way in ways:
-            for half in range(2):
+            for half in range(PIECES):
                 sent(old_msg, slot, way, half)
 
     @pl.when(z < chips - 1)
@@ -807,10 +847,10 @@
             held(pad, CMP_STRIDE * vw),
             held(n_kv, CORES, width, half_k),
             held(n_kv, CORES, half_v, vw),
-            held(chunks, width),
-            held(chunks, vw),
-            held(n_seq, chunks, width),
-            held(n_seq, chunks, vw),
+            held(2 * chunks + chunks // 2, vw),
+            held(n_seq, 2 * chunks + chunks // 2, vw),
+            held(n_seq * chunks, width),
+            held(n_seq * chunks, vw),
             held(tile_rows, width),
             pltpu.VMEM((tile_rows, heads * branches), jnp.float32),
             pltpu.VMEM((tile_rows, vw), jnp.float32),
@@ -819,15 +859,15 @@
             held(picks * SEL_BLOCK, width),
             held(picks * SEL_BLOCK, vw),
             dma((6 + 2 * CORES,)),
-            dma((2,)),
-            dma((3, n_seq, 3, 2)),
-            dma((n_seq, 3, 2)),
+            dma,
+            dma((3, n_seq, 3, PIECES)),
+            dma((n_seq, 3, PIECES)),
             dma((3, n_seq, 3)),
             dma((n_seq, 3)),
             dma((2 * (n_kv - 1), 2)),
             dma((n_kv, CORES, 2)),
-            dma((n_seq - 1, 2)),
-            dma((n_seq, 2)),
+            dma((n_seq - 1,)),
+            dma((n_seq,)),
         ],
         compiler_params=pltpu.CompilerParams(
             collective_id=0, has_side_effects=True, vmem_limit_bytes=60 << 20

time: 73.4 us -> 69.5 us (0.947); the launches traced: 72 us -> 69.4 us
  Pallas kernels: 70.1 us -> 67.5 us
    pallas_call x1, Pallas kernels: 70.1 us -> 67.5 us  [shards_gathered(): pl.pallas_call(functools.partial(fused_kernel, n_seq, n_kv, tiles), out_s...]
where the time goes in v3:
time: 69.5 us; the launch traced here: 69.4 us
  Pallas kernels  67.5 us (97%)
  local copies, waits for them, and re-layouts  1.88 us (3%)
    pallas_call x1, Pallas kernels, shards_gathered(): pl.pallas_call(functools.partial(fused_kernel, n_seq, n_kv, tiles), out_s...  67.5 us
    unnamed x1, local copies, waits for them, and re-layouts  1.88 us

profile of v3, /device:TPU:1, one launch (start us, length us, event | category | flops | bytes accessed | tf_op | source)
XLA Modules:
  0.0 69.4 jit_solution(4999326641397156682)
XLA Ops:
  0.0 67.5 %shard_map.91 = bf16[128,2048]{1,0:T(8,128)(2,1)} custom-call(s32[4,16]{1,0:T(4,128)} %bitcast.15, bf16[128,3072]{1,0:T(8,128)(2,1)} %q.1, bf16[192,1024]{1,0:T(8,128)(2,1)} %bitcast.10, bf16[16,64,128]{2,1,0:T(8,128)(2,1)} %bitcast.11, bf16[192,128]{1,0:T(8,128)(2,1)} %bitcast.12, bf16[2,64,128]{2,1,0:T(8,128)(2,1)} %bitcast.13, bf16[192,1536]{1,0:T(8,128)(2,1)} %bitcast.9, ...), custom_call_target="tpu_custom_call" | custom-call | tf_op jit(solution)/shard_map/pallas_call | solution.py:827
  67.5 1.9 %copy.11 = bf16[128,2048]{1,0:T(8,128)(2,1)} copy(bf16[128,2048]{1,0:T(8,128)(2,1)} %shard_map.91) | data formatting | bytes 1048576
